TPU v7x, 512 devices: a whole 4x4x16 slice. The times are simulated.
512 devices in a mesh: slab: 32 (over y, x, core), cross: 16 (over z).
Axes of the slice: x: 4, y: 4, z: 16, core: 2. Of those that a mesh axis runs over, the one named last changes fastest.
Arguments:
- pore_mask: int32 [128, 256, 128], P('slab', 'cross'), may hold values from 0 to 1, as said below
- phase_labels: int32 [128, 256, 128], P('slab', 'cross'), may hold values 0 or 1
- velocity: float32 [3, 128, 256, 128], P(None, 'slab', 'cross'), may hold values from -0.3 to 0.3
Outputs:
- phase_field: float32 [128, 256, 128], P('slab', 'cross')
- populations: float32 [19, 128, 256, 128], P(None, 'slab', 'cross')
Inputs may be any that keep to these rules, and one draw needn't show every extreme that they name: `pore_mask`: 1 marks a pore voxel. `phase_labels`: 1 marks the first fluid.
All inputs are finite; a program needn't handle non-finite values. No bound on the sum of `phase_labels` on one device may be relied on, other than what follows from the above.
Results may differ from a plain program's by a relative error of at most 0.0003.
Values sent between devices are 32-bit elements; how exact they have to be, the bound alone decides.
No kernel may reach another device: no remote copies, remote signals or barrier semaphores. Data moves between devices by JAX's collectives and lax.ppermute only.
A program may use at most 64 MiB of HBM per device.

v0:
```python
import jax
import jax.numpy as jnp
from jax import lax
from jax.sharding import PartitionSpec as P

STEPS = 4


lattice_dirs = [
    (0, 0, 0),
    (1, 0, 0),
    (-1, 0, 0),
    (0, 1, 0),
    (0, -1, 0),
    (0, 0, 1),
    (0, 0, -1),
    (1, 1, 0),
    (-1, -1, 0),
    (1, -1, 0),
    (-1, 1, 0),
    (1, 0, 1),
    (-1, 0, -1),
    (1, 0, -1),
    (-1, 0, 1),
    (0, 1, 1),
    (0, -1, -1),
    (0, 1, -1),
    (0, -1, 1),
]
lattice_weights = [1.0 / 3.0] + [1.0 / 18.0] * 6 + [1.0 / 36.0] * 12
tension_offsets = [-1.0 / 3.0] + [1.0 / 18.0] * 6 + [1.0 / 36.0] * 12
phase_weights = [0.25] + [0.125] * 6
relax_red = 1.0
relax_blue = 0.7
tension = 0.1
segregation = 0.7
driving = 0.001


def padded_2(array, sides, width):
    for axis, dim in sides:
        devices, length = (lax.axis_size(axis), array.shape[dim])
        up = [(i, (i + 1) % devices) for i in range(devices)]
        down = [(j, i) for i, j in up]
        last = lax.slice_in_dim(array, length - width, length, axis=dim)
        first = lax.slice_in_dim(array, 0, width, axis=dim)
        before = lax.ppermute(last, axis, up)
        after = lax.ppermute(first, axis, down)
        array = jnp.concatenate([before, array, after], axis=dim)
    return array


def opposite(member):
    if member == 0:
        return 0
    return member + 1 if member % 2 == 1 else member - 1


def project(heading, vectors):
    summed = jnp.zeros_like(vectors[0])
    for component in range(3):
        if heading[component] != 0:
            summed = summed + float(heading[component]) * vectors[component]
    return summed


def momentum_equilibrium(density, velocity):
    speed_sq = velocity[0] * velocity[0] + velocity[1] * velocity[1] + velocity[2] * velocity[2]
    result = []
    for member in range(19):
        flow_dot = project(lattice_dirs[member], velocity)
        result.append(
            lattice_weights[member]
            * density
            * (1.0 + 3.0 * flow_dot + 4.5 * flow_dot * flow_dot - 1.5 * speed_sq)
        )
    return result


def phase_update(red_mass, blue_mass, velocity, normal):
    red_pops = []
    blue_pops = []
    if normal is not None:
        mixed = segregation * red_mass * blue_mass / (red_mass + blue_mass)
    for member in range(7):
        heading = lattice_dirs[member]
        flow_dot = project(heading, velocity)
        red_new = red_mass * (1.0 + 4.0 * flow_dot)
        blue_new = blue_mass * (1.0 + 4.0 * flow_dot)
        if normal is not None:
            bias = mixed * project(heading, normal)
            red_new = red_new + bias
            blue_new = blue_new - bias
        red_pops.append(phase_weights[member] * red_new)
        blue_pops.append(phase_weights[member] * blue_new)
    return (red_pops, blue_pops)


def moments(populations, red_pops, blue_pops):
    density = populations[0]
    for member in range(1, 19):
        density = density + populations[member]
    velocity = []
    for component in range(3):
        summed = jnp.zeros_like(density)
        for member in range(19):
            offset = lattice_dirs[member][component]
            if offset != 0:
                summed = summed + float(offset) * populations[member]
        velocity.append(summed / density)
    red_mass = red_pops[0]
    blue_mass = blue_pops[0]
    for member in range(1, 7):
        red_mass = red_mass + red_pops[member]
        blue_mass = blue_mass + blue_pops[member]
    colour = (red_mass - blue_mass) / (red_mass + blue_mass)
    return (density, velocity, red_mass, blue_mass, colour)


def colour_gradient(neighbour, template):
    gradient = [jnp.zeros_like(template), jnp.zeros_like(template), jnp.zeros_like(template)]
    for member in range(1, 19):
        heading = lattice_dirs[member]
        nearby = neighbour(heading)
        for component in range(3):
            if heading[component] != 0:
                gradient[component] = (
                    gradient[component]
                    + 3.0 * lattice_weights[member] * heading[component] * nearby
                )
    return gradient


def collide(populations, density, velocity, red_mass, blue_mass, colour, gradient):
    relax = 0.5 * (1.0 + colour) * relax_red + 0.5 * (1.0 - colour) * relax_blue
    omega = 1.0 / relax
    equilibrium = momentum_equilibrium(density, velocity)
    grad_sq = gradient[0] * gradient[0] + gradient[1] * gradient[1] + gradient[2] * gradient[2]
    length = jnp.maximum(jnp.sqrt(grad_sq), 0.5)
    normal = [gradient[0] / length, gradient[1] / length, gradient[2] / length]
    post = []
    for member in range(19):
        heading = lattice_dirs[member]
        along_grad = project(heading, gradient)
        tensile = tension * (
            lattice_weights[member] * along_grad * along_grad - tension_offsets[member] * grad_sq
        )
        forcing = 3.0 * lattice_weights[member] * driving * heading[0] * density
        post.append(
            populations[member]
            - omega * (populations[member] - equilibrium[member])
            + tensile
            + forcing
        )
    red_post, blue_post = phase_update(red_mass, blue_mass, velocity, normal)
    return (post, red_post, blue_post)


def shifted(padded, heading, width_x, width_y):
    block = padded[
        1 - heading[0] : 1 - heading[0] + width_x, 1 - heading[1] : 1 - heading[1] + width_y, :
    ]
    return jnp.roll(block, heading[2], axis=-1)


def stream_rim(padded, first, post, prior, rim_mask, pore, count):
    width_x, width_y = (pore.shape[0], pore.shape[1])
    result = []
    for member in range(count):
        heading = lattice_dirs[member]
        pulled = shifted(padded[first + member], heading, width_x, width_y)
        opened = shifted(rim_mask, heading, width_x, width_y)
        moved = jnp.where(opened > 0, pulled, post[opposite(member)])
        result.append(jnp.where(pore > 0, moved, prior[member]))
    return result


def shards(pore_mask, phase_labels, velocity):
    width_x, width_y = (pore_mask.shape[0], pore_mask.shape[1])
    rim_mask = padded_2(pore_mask, (("slab", 0), ("cross", 1)), 1)
    labels = phase_labels.astype(jnp.float32)
    start_vel = [velocity[0], velocity[1], velocity[2]]
    populations = momentum_equilibrium(jnp.ones_like(labels), start_vel)
    red_pops, blue_pops = phase_update(labels, 1.0 - labels, start_vel, None)
    for iteration in range(STEPS):
        density, flow, red_mass, blue_mass, colour = moments(populations, red_pops, blue_pops)
        tinted = jnp.where(pore_mask > 0, colour, 0.0)
        padded_colour = padded_2(tinted, (("slab", 0), ("cross", 1)), 1)

        def neighbour(heading):
            return shifted(padded_colour, (-heading[0], -heading[1], -heading[2]), width_x, width_y)

        gradient = colour_gradient(neighbour, tinted)
        post, red_post, blue_post = collide(
            populations, density, flow, red_mass, blue_mass, colour, gradient
        )
        stacked = jnp.stack(post + red_post + blue_post)
        padded = padded_2(stacked, (("slab", 1), ("cross", 2)), 1)
        populations = stream_rim(padded, 0, post, populations, rim_mask, pore_mask, 19)
        red_pops = stream_rim(padded, 19, red_post, red_pops, rim_mask, pore_mask, 7)
        blue_pops = stream_rim(padded, 26, blue_post, blue_pops, rim_mask, pore_mask, 7)
    density, flow, red_mass, blue_mass, colour = moments(populations, red_pops, blue_pops)
    return (jnp.where(pore_mask > 0, colour, 0.0), jnp.stack(populations))


def solution(mesh):
    in_specs = (P("slab", "cross", None), P("slab", "cross", None), P(None, "slab", "cross", None))
    out_specs = (P("slab", "cross", None), P(None, "slab", "cross", None))
    return jax.shard_map(shards, mesh=mesh, in_specs=in_specs, out_specs=out_specs, check_vma=False)
```

profile of v0, /device:TPU:32, one launch (start us, length us, event | category | flops | bytes accessed | tf_op | source)
XLA Modules:
  0.0 225.8 jit_solution(17389814788890304767)
XLA Ops:
  1.6 2.1 collective-permute-start.1
  3.6 7.0 %collective-permute-start = (f32[1,16,128]{2,1,0:T(8,128)S(1)}, f32[1,16,128]{2,1,0:T(8,128)S(1)}, u32[]{:S(2)}, u32[]{:S(2)}) collective-permute-start(f32[1,16,128]{2,1,0:T(8,128)S(1)} %get-tuple-element.695), channel_id=1, source_target_pairs={{16,0},{32,16},{48,32},{64,48},{80,64},{96,80},{112,96},{128,112},... | collective-permute-start | bytes 24584 | tf_op jit(solution)/shard_map/ppermute | solution.py:48
  11.3 1.9 collective-permute-start.8
  13.2 7.0 %collective-permute-start.9 = (s32[1,16,128]{2,1,0:T(8,128)S(1)}, s32[1,16,128]{2,1,0:T(8,128)S(1)}, u32[]{:S(2)}, u32[]{:S(2)}) collective-permute-start(s32[1,16,128]{2,1,0:T(8,128)S(1)} %get-tuple-element.685), channel_id=1, source_target_pairs={{16,0},{32,16},{48,32},{64,48},{80,64},{96,80},{112,96},{128,112},... | collective-permute-start | bytes 24584 | tf_op jit(solution)/shard_map/ppermute | solution.py:48
  23.0 3.8 %collective-permute-start.3 = (f32[6,1,128]{2,1,0:T(1,128)S(1)}, f32[6,1,128]{2,1,0:T(1,128)S(1)}, u32[]{:S(2)}, u32[]{:S(2)}) collective-permute-start(f32[6,1,128]{2,1,0:T(1,128)S(1)} %get-tuple-element.622), channel_id=1, source_target_pairs={{0,1},{1,2},{2,3},{3,4},{4,5},{5,6},{6,7},{7,8},{8,9},{9,10},{10,1... | collective-permute-start | bytes 9224 | tf_op jit(solution)/shard_map/ppermute | solution.py:47
  26.8 5.5 %collective-permute-start.2 = (f32[6,1,128]{2,1,0:T(1,128)S(1)}, f32[6,1,128]{2,1,0:T(1,128)S(1)}, u32[]{:S(2)}, u32[]{:S(2)}) collective-permute-start(f32[6,1,128]{2,1,0:T(1,128)S(1)} %get-tuple-element.623), channel_id=1, source_target_pairs={{1,0},{2,1},{3,2},{4,3},{5,4},{6,5},{7,6},{8,7},{9,8},{10,9},{11,1... | collective-permute-start | bytes 9224 | tf_op jit(solution)/shard_map/ppermute | solution.py:48
  32.3 1.9 collective-permute-start.10
  34.2 6.1 %collective-permute-start.11 = (s32[6,1,128]{2,1,0:T(1,128)S(1)}, s32[6,1,128]{2,1,0:T(1,128)S(1)}, u32[]{:S(2)}, u32[]{:S(2)}) collective-permute-start(s32[6,1,128]{2,1,0:T(1,128)S(1)} %get-tuple-element.618), channel_id=1, source_target_pairs={{1,0},{2,1},{3,2},{4,3},{5,4},{6,5},{7,6},{8,7},{9,8},{10,9},{11,1... | collective-permute-start | bytes 9224 | tf_op jit(solution)/shard_map/ppermute | solution.py:48
  42.4 1.9 collective-permute-start.5
  44.4 2.4 %collective-permute-start.4 = (f32[33,1,16,128]{3,2,1,0:T(8,128)S(1)}, f32[33,1,16,128]{3,2,1,0:T(8,128)S(1)}, u32[]{:S(2)}, u32[]{:S(2)}) collective-permute-start(f32[33,1,16,128]{3,2,1,0:T(8,128)S(1)} %get-tuple-element.560), channel_id=1, source_target_pairs={{0,16},{16,32},{32,48},{48,64},{64,80},{80,96},{96,112},{112,128},... | collective-permute-start | bytes 811016 | tf_op jit(solution)/shard_map/ppermute | solution.py:47
  46.9 1.4 collective-permute-done.5
  48.3 7.1 %collective-permute-done.4 = f32[33,1,16,128]{3,2,1,0:T(8,128)S(1)} collective-permute-done((f32[33,1,16,128]{3,2,1,0:T(8,128)S(1)}, f32[33,1,16,128]{3,2,1,0:T(8,128)S(1)}, u32[]{:S(2)}, u32[]{:S(2)}) %collective-permute-start.4) | collective-permute-done | bytes 270368 | tf_op jit(solution)/shard_map/ppermute | solution.py:47
  55.6 5.1 %collective-permute-start.7 = (f32[33,6,1,128]{3,2,1,0:T(1,128)S(1)}, f32[33,6,1,128]{3,2,1,0:T(1,128)S(1)}, u32[]{:S(2)}, u32[]{:S(2)}) collective-permute-start(f32[33,6,1,128]{3,2,1,0:T(1,128)S(1)} %get-tuple-element.553), channel_id=1, source_target_pairs={{1,0},{2,1},{3,2},{4,3},{5,4},{6,5},{7,6},{8,7},{9,8},{10,9},{11,1... | collective-permute-start | bytes 304136 | tf_op jit(solution)/shard_map/ppermute | solution.py:48
  60.7 1.9 collective-permute-start.6
  63.0 4.3 %collective-permute-done.6 = f32[33,6,1,128]{3,2,1,0:T(1,128)S(1)} collective-permute-done((f32[33,6,1,128]{3,2,1,0:T(1,128)S(1)}, f32[33,6,1,128]{3,2,1,0:T(1,128)S(1)}, u32[]{:S(2)}, u32[]{:S(2)}) %collective-permute-start.6) | collective-permute-done | bytes 101408 | tf_op jit(solution)/shard_map/ppermute | solution.py:47
  69.1 1.9 collective-permute-start.13
  71.0 7.0 %collective-permute-start.12 = (f32[1,16,128]{2,1,0:T(8,128)S(1)}, f32[1,16,128]{2,1,0:T(8,128)S(1)}, u32[]{:S(2)}, u32[]{:S(2)}) collective-permute-start(f32[1,16,128]{2,1,0:T(8,128)S(1)} %get-tuple-element.676), channel_id=1, source_target_pairs={{16,0},{32,16},{48,32},{64,48},{80,64},{96,80},{112,96},{128,112},... | collective-permute-start | bytes 24584 | tf_op jit(solution)/shard_map/ppermute | solution.py:48
  79.3 1.9 collective-permute-start.15
  81.2 3.9 %collective-permute-start.14 = (f32[6,1,128]{2,1,0:T(1,128)S(1)}, f32[6,1,128]{2,1,0:T(1,128)S(1)}, u32[]{:S(2)}, u32[]{:S(2)}) collective-permute-start(f32[6,1,128]{2,1,0:T(1,128)S(1)} %get-tuple-element.617), channel_id=1, source_target_pairs={{1,0},{2,1},{3,2},{4,3},{5,4},{6,5},{7,6},{8,7},{9,8},{10,9},{11,1... | collective-permute-start | bytes 9224 | tf_op jit(solution)/shard_map/ppermute | solution.py:48
  88.9 5.8 %collective-permute-start.17 = (f32[33,1,16,128]{3,2,1,0:T(8,128)S(1)}, f32[33,1,16,128]{3,2,1,0:T(8,128)S(1)}, u32[]{:S(2)}, u32[]{:S(2)}) collective-permute-start(f32[33,1,16,128]{3,2,1,0:T(8,128)S(1)} %get-tuple-element.559), channel_id=1, source_target_pairs={{16,0},{32,16},{48,32},{64,48},{80,64},{96,80},{112,96},{128,112},... | collective-permute-start | bytes 811016 | tf_op jit(solution)/shard_map/ppermute | solution.py:48
  94.7 1.9 collective-permute-start.16
  96.7 2.0 collective-permute-done.17
  98.7 7.1 %collective-permute-done.16 = f32[33,1,16,128]{3,2,1,0:T(8,128)S(1)} collective-permute-done((f32[33,1,16,128]{3,2,1,0:T(8,128)S(1)}, f32[33,1,16,128]{3,2,1,0:T(8,128)S(1)}, u32[]{:S(2)}, u32[]{:S(2)}) %collective-permute-start.16) | collective-permute-done | bytes 270368 | tf_op jit(solution)/shard_map/ppermute | solution.py:47
  106.0 4.9 %collective-permute-start.19 = (f32[33,6,1,128]{3,2,1,0:T(1,128)S(1)}, f32[33,6,1,128]{3,2,1,0:T(1,128)S(1)}, u32[]{:S(2)}, u32[]{:S(2)}) collective-permute-start(f32[33,6,1,128]{3,2,1,0:T(1,128)S(1)} %get-tuple-element.551), channel_id=1, source_target_pairs={{1,0},{2,1},{3,2},{4,3},{5,4},{6,5},{7,6},{8,7},{9,8},{10,9},{11,1... | collective-permute-start | bytes 304136 | tf_op jit(solution)/shard_map/ppermute | solution.py:48
  110.8 1.9 collective-permute-start.18
  113.1 5.5 %collective-permute-done.18 = f32[33,6,1,128]{3,2,1,0:T(1,128)S(1)} collective-permute-done((f32[33,6,1,128]{3,2,1,0:T(1,128)S(1)}, f32[33,6,1,128]{3,2,1,0:T(1,128)S(1)}, u32[]{:S(2)}, u32[]{:S(2)}) %collective-permute-start.18) | collective-permute-done | bytes 101408 | tf_op jit(solution)/shard_map/ppermute | solution.py:47
  119.7 1.9 collective-permute-start.21
  121.6 7.0 %collective-permute-start.20 = (f32[1,16,128]{2,1,0:T(8,128)S(1)}, f32[1,16,128]{2,1,0:T(8,128)S(1)}, u32[]{:S(2)}, u32[]{:S(2)}) collective-permute-start(f32[1,16,128]{2,1,0:T(8,128)S(1)} %get-tuple-element.666), channel_id=1, source_target_pairs={{16,0},{32,16},{48,32},{64,48},{80,64},{96,80},{112,96},{128,112},... | collective-permute-start | bytes 24584 | tf_op jit(solution)/shard_map/ppermute | solution.py:48
  130.0 1.9 collective-permute-start.23
  131.9 5.1 %collective-permute-start.22 = (f32[6,1,128]{2,1,0:T(1,128)S(1)}, f32[6,1,128]{2,1,0:T(1,128)S(1)}, u32[]{:S(2)}, u32[]{:S(2)}) collective-permute-start(f32[6,1,128]{2,1,0:T(1,128)S(1)} %get-tuple-element.609), channel_id=1, source_target_pairs={{1,0},{2,1},{3,2},{4,3},{5,4},{6,5},{7,6},{8,7},{9,8},{10,9},{11,1... | collective-permute-start | bytes 9224 | tf_op jit(solution)/shard_map/ppermute | solution.py:48
  140.4 6.1 %collective-permute-start.25 = (f32[33,1,16,128]{3,2,1,0:T(8,128)S(1)}, f32[33,1,16,128]{3,2,1,0:T(8,128)S(1)}, u32[]{:S(2)}, u32[]{:S(2)}) collective-permute-start(f32[33,1,16,128]{3,2,1,0:T(8,128)S(1)} %get-tuple-element.557), channel_id=1, source_target_pairs={{16,0},{32,16},{48,32},{64,48},{80,64},{96,80},{112,96},{128,112},... | collective-permute-start | bytes 811016 | tf_op jit(solution)/shard_map/ppermute | solution.py:48
  146.5 1.9 collective-permute-start.24
  148.4 2.0 collective-permute-done.25
  150.4 7.1 %collective-permute-done.24 = f32[33,1,16,128]{3,2,1,0:T(8,128)S(1)} collective-permute-done((f32[33,1,16,128]{3,2,1,0:T(8,128)S(1)}, f32[33,1,16,128]{3,2,1,0:T(8,128)S(1)}, u32[]{:S(2)}, u32[]{:S(2)}) %collective-permute-start.24) | collective-permute-done | bytes 270368 | tf_op jit(solution)/shard_map/ppermute | solution.py:47
  157.7 4.9 %collective-permute-start.27 = (f32[33,6,1,128]{3,2,1,0:T(1,128)S(1)}, f32[33,6,1,128]{3,2,1,0:T(1,128)S(1)}, u32[]{:S(2)}, u32[]{:S(2)}) collective-permute-start(f32[33,6,1,128]{3,2,1,0:T(1,128)S(1)} %get-tuple-element.549), channel_id=1, source_target_pairs={{1,0},{2,1},{3,2},{4,3},{5,4},{6,5},{7,6},{8,7},{9,8},{10,9},{11,1... | collective-permute-start | bytes 304136 | tf_op jit(solution)/shard_map/ppermute | solution.py:48
  162.6 1.9 collective-permute-start.26
  164.8 5.5 %collective-permute-done.26 = f32[33,6,1,128]{3,2,1,0:T(1,128)S(1)} collective-permute-done((f32[33,6,1,128]{3,2,1,0:T(1,128)S(1)}, f32[33,6,1,128]{3,2,1,0:T(1,128)S(1)}, u32[]{:S(2)}, u32[]{:S(2)}) %collective-permute-start.26) | collective-permute-done | bytes 101408 | tf_op jit(solution)/shard_map/ppermute | solution.py:47
  171.4 1.9 collective-permute-start.29
  173.4 7.1 %collective-permute-start.28 = (f32[1,16,128]{2,1,0:T(8,128)S(1)}, f32[1,16,128]{2,1,0:T(8,128)S(1)}, u32[]{:S(2)}, u32[]{:S(2)}) collective-permute-start(f32[1,16,128]{2,1,0:T(8,128)S(1)} %get-tuple-element.656), channel_id=1, source_target_pairs={{16,0},{32,16},{48,32},{64,48},{80,64},{96,80},{112,96},{128,112},... | collective-permute-start | bytes 24584 | tf_op jit(solution)/shard_map/ppermute | solution.py:48
  181.7 1.9 collective-permute-start.31
  183.6 5.1 %collective-permute-start.30 = (f32[6,1,128]{2,1,0:T(1,128)S(1)}, f32[6,1,128]{2,1,0:T(1,128)S(1)}, u32[]{:S(2)}, u32[]{:S(2)}) collective-permute-start(f32[6,1,128]{2,1,0:T(1,128)S(1)} %get-tuple-element.605), channel_id=1, source_target_pairs={{1,0},{2,1},{3,2},{4,3},{5,4},{6,5},{7,6},{8,7},{9,8},{10,9},{11,1... | collective-permute-start | bytes 9224 | tf_op jit(solution)/shard_map/ppermute | solution.py:48
  192.1 6.1 %collective-permute-start.33 = (f32[33,1,16,128]{3,2,1,0:T(8,128)S(1)}, f32[33,1,16,128]{3,2,1,0:T(8,128)S(1)}, u32[]{:S(2)}, u32[]{:S(2)}) collective-permute-start(f32[33,1,16,128]{3,2,1,0:T(8,128)S(1)} %get-tuple-element.555), channel_id=1, source_target_pairs={{16,0},{32,16},{48,32},{64,48},{80,64},{96,80},{112,96},{128,112},... | collective-permute-start | bytes 811016 | tf_op jit(solution)/shard_map/ppermute | solution.py:48
  198.2 1.9 collective-permute-start.32
  200.1 2.0 collective-permute-done.33
  202.2 7.1 %collective-permute-done.32 = f32[33,1,16,128]{3,2,1,0:T(8,128)S(1)} collective-permute-done((f32[33,1,16,128]{3,2,1,0:T(8,128)S(1)}, f32[33,1,16,128]{3,2,1,0:T(8,128)S(1)}, u32[]{:S(2)}, u32[]{:S(2)}) %collective-permute-start.32) | collective-permute-done | bytes 270368 | tf_op jit(solution)/shard_map/ppermute | solution.py:47
  209.4 4.9 %collective-permute-start.35 = (f32[33,6,1,128]{3,2,1,0:T(1,128)S(1)}, f32[33,6,1,128]{3,2,1,0:T(1,128)S(1)}, u32[]{:S(2)}, u32[]{:S(2)}) collective-permute-start(f32[33,6,1,128]{3,2,1,0:T(1,128)S(1)} %get-tuple-element.547), channel_id=1, source_target_pairs={{1,0},{2,1},{3,2},{4,3},{5,4},{6,5},{7,6},{8,7},{9,8},{10,9},{11,1... | collective-permute-start | bytes 304136 | tf_op jit(solution)/shard_map/ppermute | solution.py:48
  214.3 1.9 collective-permute-start.34
  216.5 5.5 %collective-permute-done.34 = f32[33,6,1,128]{3,2,1,0:T(1,128)S(1)} collective-permute-done((f32[33,6,1,128]{3,2,1,0:T(1,128)S(1)}, f32[33,6,1,128]{3,2,1,0:T(1,128)S(1)}, u32[]{:S(2)}, u32[]{:S(2)}) %collective-permute-start.34) | collective-permute-done | bytes 101408 | tf_op jit(solution)/shard_map/ppermute | solution.py:47
  (365 shorter events, 29.2 us)
Async XLA Ops:
  1.5 39.2 %copy-start = (f32[3,4,16,128]{3,2,1,0:T(8,128)S(1)}, f32[3,4,16,128]{3,2,1,0:T(8,128)}, u32[]{:S(2)}) copy-start(f32[3,4,16,128]{3,2,1,0:T(8,128)} %param.5) | copy-start | bytes 294916
  1.6 21.4 %collective-permute-start.1 = (f32[1,16,128]{2,1,0:T(8,128)S(1)}, f32[1,16,128]{2,1,0:T(8,128)S(1)}, u32[]{:S(2)}, u32[]{:S(2)}) collective-permute-start(f32[1,16,128]{2,1,0:T(8,128)S(1)} %get-tuple-element.696), channel_id=1, source_target_pairs={{0,16},{16,32},{32,48},{48,64},{64,80},{80,96},{96,112},{112,128},... | collective-permute-start | bytes 24584 | tf_op jit(solution)/shard_map/ppermute | solution.py:47
  3.6 19.3 %collective-permute-start = (f32[1,16,128]{2,1,0:T(8,128)S(1)}, f32[1,16,128]{2,1,0:T(8,128)S(1)}, u32[]{:S(2)}, u32[]{:S(2)}) collective-permute-start(f32[1,16,128]{2,1,0:T(8,128)S(1)} %get-tuple-element.695), channel_id=1, source_target_pairs={{16,0},{32,16},{48,32},{64,48},{80,64},{96,80},{112,96},{128,112},... | collective-permute-start | bytes 24584 | tf_op jit(solution)/shard_map/ppermute | solution.py:48
  11.3 10.7 %collective-permute-start.8 = (s32[1,16,128]{2,1,0:T(8,128)S(1)}, s32[1,16,128]{2,1,0:T(8,128)S(1)}, u32[]{:S(2)}, u32[]{:S(2)}) collective-permute-start(s32[1,16,128]{2,1,0:T(8,128)S(1)} %get-tuple-element.686), channel_id=1, source_target_pairs={{0,16},{16,32},{32,48},{48,64},{64,80},{80,96},{96,112},{112,128},... | collective-permute-start | bytes 24584 | tf_op jit(solution)/shard_map/ppermute | solution.py:47
  13.2 19.1 %collective-permute-start.9 = (s32[1,16,128]{2,1,0:T(8,128)S(1)}, s32[1,16,128]{2,1,0:T(8,128)S(1)}, u32[]{:S(2)}, u32[]{:S(2)}) collective-permute-start(s32[1,16,128]{2,1,0:T(8,128)S(1)} %get-tuple-element.685), channel_id=1, source_target_pairs={{16,0},{32,16},{48,32},{64,48},{80,64},{96,80},{112,96},{128,112},... | collective-permute-start | bytes 24584 | tf_op jit(solution)/shard_map/ppermute | solution.py:48
  23.0 17.5 %collective-permute-start.3 = (f32[6,1,128]{2,1,0:T(1,128)S(1)}, f32[6,1,128]{2,1,0:T(1,128)S(1)}, u32[]{:S(2)}, u32[]{:S(2)}) collective-permute-start(f32[6,1,128]{2,1,0:T(1,128)S(1)} %get-tuple-element.622), channel_id=1, source_target_pairs={{0,1},{1,2},{2,3},{3,4},{4,5},{5,6},{6,7},{7,8},{8,9},{9,10},{10,1... | collective-permute-start | bytes 9224 | tf_op jit(solution)/shard_map/ppermute | solution.py:47
  26.8 13.7 %collective-permute-start.2 = (f32[6,1,128]{2,1,0:T(1,128)S(1)}, f32[6,1,128]{2,1,0:T(1,128)S(1)}, u32[]{:S(2)}, u32[]{:S(2)}) collective-permute-start(f32[6,1,128]{2,1,0:T(1,128)S(1)} %get-tuple-element.623), channel_id=1, source_target_pairs={{1,0},{2,1},{3,2},{4,3},{5,4},{6,5},{7,6},{8,7},{9,8},{10,9},{11,1... | collective-permute-start | bytes 9224 | tf_op jit(solution)/shard_map/ppermute | solution.py:48
  32.3 30.4 %collective-permute-start.10 = (s32[6,1,128]{2,1,0:T(1,128)S(1)}, s32[6,1,128]{2,1,0:T(1,128)S(1)}, u32[]{:S(2)}, u32[]{:S(2)}) collective-permute-start(s32[6,1,128]{2,1,0:T(1,128)S(1)} %get-tuple-element.619), channel_id=1, source_target_pairs={{0,1},{1,2},{2,3},{3,4},{4,5},{5,6},{6,7},{7,8},{8,9},{9,10},{10,1... | collective-permute-start | bytes 9224 | tf_op jit(solution)/shard_map/ppermute | solution.py:47
  34.2 28.4 %collective-permute-start.11 = (s32[6,1,128]{2,1,0:T(1,128)S(1)}, s32[6,1,128]{2,1,0:T(1,128)S(1)}, u32[]{:S(2)}, u32[]{:S(2)}) collective-permute-start(s32[6,1,128]{2,1,0:T(1,128)S(1)} %get-tuple-element.618), channel_id=1, source_target_pairs={{1,0},{2,1},{3,2},{4,3},{5,4},{6,5},{7,6},{8,7},{9,8},{10,9},{11,1... | collective-permute-start | bytes 9224 | tf_op jit(solution)/shard_map/ppermute | solution.py:48
  42.4 5.9 %collective-permute-start.5 = (f32[33,1,16,128]{3,2,1,0:T(8,128)S(1)}, f32[33,1,16,128]{3,2,1,0:T(8,128)S(1)}, u32[]{:S(2)}, u32[]{:S(2)}) collective-permute-start(f32[33,1,16,128]{3,2,1,0:T(8,128)S(1)} %get-tuple-element.561), channel_id=1, source_target_pairs={{16,0},{32,16},{48,32},{64,48},{80,64},{96,80},{112,96},{128,112},... | collective-permute-start | bytes 811016 | tf_op jit(solution)/shard_map/ppermute | solution.py:48
  44.4 11.1 %collective-permute-start.4 = (f32[33,1,16,128]{3,2,1,0:T(8,128)S(1)}, f32[33,1,16,128]{3,2,1,0:T(8,128)S(1)}, u32[]{:S(2)}, u32[]{:S(2)}) collective-permute-start(f32[33,1,16,128]{3,2,1,0:T(8,128)S(1)} %get-tuple-element.560), channel_id=1, source_target_pairs={{0,16},{16,32},{32,48},{48,64},{64,80},{80,96},{96,112},{112,128},... | collective-permute-start | bytes 811016 | tf_op jit(solution)/shard_map/ppermute | solution.py:47
  55.6 7.4 %collective-permute-start.7 = (f32[33,6,1,128]{3,2,1,0:T(1,128)S(1)}, f32[33,6,1,128]{3,2,1,0:T(1,128)S(1)}, u32[]{:S(2)}, u32[]{:S(2)}) collective-permute-start(f32[33,6,1,128]{3,2,1,0:T(1,128)S(1)} %get-tuple-element.553), channel_id=1, source_target_pairs={{1,0},{2,1},{3,2},{4,3},{5,4},{6,5},{7,6},{8,7},{9,8},{10,9},{11,1... | collective-permute-start | bytes 304136 | tf_op jit(solution)/shard_map/ppermute | solution.py:48
  60.7 6.5 %collective-permute-start.6 = (f32[33,6,1,128]{3,2,1,0:T(1,128)S(1)}, f32[33,6,1,128]{3,2,1,0:T(1,128)S(1)}, u32[]{:S(2)}, u32[]{:S(2)}) collective-permute-start(f32[33,6,1,128]{3,2,1,0:T(1,128)S(1)} %get-tuple-element.552), channel_id=1, source_target_pairs={{0,1},{1,2},{2,3},{3,4},{4,5},{5,6},{6,7},{7,8},{8,9},{9,10},{10,1... | collective-permute-start | bytes 304136 | tf_op jit(solution)/shard_map/ppermute | solution.py:47
  68.1 0.8 copy-start.1
  69.1 9.9 %collective-permute-start.13 = (f32[1,16,128]{2,1,0:T(8,128)S(1)}, f32[1,16,128]{2,1,0:T(8,128)S(1)}, u32[]{:S(2)}, u32[]{:S(2)}) collective-permute-start(f32[1,16,128]{2,1,0:T(8,128)S(1)} %get-tuple-element.677), channel_id=1, source_target_pairs={{0,16},{16,32},{32,48},{48,64},{64,80},{80,96},{96,112},{112,128},... | collective-permute-start | bytes 24584 | tf_op jit(solution)/shard_map/ppermute | solution.py:47
  71.0 8.3 %collective-permute-start.12 = (f32[1,16,128]{2,1,0:T(8,128)S(1)}, f32[1,16,128]{2,1,0:T(8,128)S(1)}, u32[]{:S(2)}, u32[]{:S(2)}) collective-permute-start(f32[1,16,128]{2,1,0:T(8,128)S(1)} %get-tuple-element.676), channel_id=1, source_target_pairs={{16,0},{32,16},{48,32},{64,48},{80,64},{96,80},{112,96},{128,112},... | collective-permute-start | bytes 24584 | tf_op jit(solution)/shard_map/ppermute | solution.py:48
  79.3 6.0 %collective-permute-start.15 = (f32[6,1,128]{2,1,0:T(1,128)S(1)}, f32[6,1,128]{2,1,0:T(1,128)S(1)}, u32[]{:S(2)}, u32[]{:S(2)}) collective-permute-start(f32[6,1,128]{2,1,0:T(1,128)S(1)} %get-tuple-element.616), channel_id=1, source_target_pairs={{0,1},{1,2},{2,3},{3,4},{4,5},{5,6},{6,7},{7,8},{8,9},{9,10},{10,1... | collective-permute-start | bytes 9224 | tf_op jit(solution)/shard_map/ppermute | solution.py:47
  81.2 5.5 %collective-permute-start.14 = (f32[6,1,128]{2,1,0:T(1,128)S(1)}, f32[6,1,128]{2,1,0:T(1,128)S(1)}, u32[]{:S(2)}, u32[]{:S(2)}) collective-permute-start(f32[6,1,128]{2,1,0:T(1,128)S(1)} %get-tuple-element.617), channel_id=1, source_target_pairs={{1,0},{2,1},{3,2},{4,3},{5,4},{6,5},{7,6},{8,7},{9,8},{10,9},{11,1... | collective-permute-start | bytes 9224 | tf_op jit(solution)/shard_map/ppermute | solution.py:48
  88.9 9.8 %collective-permute-start.17 = (f32[33,1,16,128]{3,2,1,0:T(8,128)S(1)}, f32[33,1,16,128]{3,2,1,0:T(8,128)S(1)}, u32[]{:S(2)}, u32[]{:S(2)}) collective-permute-start(f32[33,1,16,128]{3,2,1,0:T(8,128)S(1)} %get-tuple-element.559), channel_id=1, source_target_pairs={{16,0},{32,16},{48,32},{64,48},{80,64},{96,80},{112,96},{128,112},... | collective-permute-start | bytes 811016 | tf_op jit(solution)/shard_map/ppermute | solution.py:48
  94.7 11.1 %collective-permute-start.16 = (f32[33,1,16,128]{3,2,1,0:T(8,128)S(1)}, f32[33,1,16,128]{3,2,1,0:T(8,128)S(1)}, u32[]{:S(2)}, u32[]{:S(2)}) collective-permute-start(f32[33,1,16,128]{3,2,1,0:T(8,128)S(1)} %get-tuple-element.558), channel_id=1, source_target_pairs={{0,16},{16,32},{32,48},{48,64},{64,80},{80,96},{96,112},{112,128},... | collective-permute-start | bytes 811016 | tf_op jit(solution)/shard_map/ppermute | solution.py:47
  106.0 7.1 %collective-permute-start.19 = (f32[33,6,1,128]{3,2,1,0:T(1,128)S(1)}, f32[33,6,1,128]{3,2,1,0:T(1,128)S(1)}, u32[]{:S(2)}, u32[]{:S(2)}) collective-permute-start(f32[33,6,1,128]{3,2,1,0:T(1,128)S(1)} %get-tuple-element.551), channel_id=1, source_target_pairs={{1,0},{2,1},{3,2},{4,3},{5,4},{6,5},{7,6},{8,7},{9,8},{10,9},{11,1... | collective-permute-start | bytes 304136 | tf_op jit(solution)/shard_map/ppermute | solution.py:48
  110.8 7.7 %collective-permute-start.18 = (f32[33,6,1,128]{3,2,1,0:T(1,128)S(1)}, f32[33,6,1,128]{3,2,1,0:T(1,128)S(1)}, u32[]{:S(2)}, u32[]{:S(2)}) collective-permute-start(f32[33,6,1,128]{3,2,1,0:T(1,128)S(1)} %get-tuple-element.550), channel_id=1, source_target_pairs={{0,1},{1,2},{2,3},{3,4},{4,5},{5,6},{6,7},{7,8},{8,9},{9,10},{10,1... | collective-permute-start | bytes 304136 | tf_op jit(solution)/shard_map/ppermute | solution.py:47
  119.7 9.8 %collective-permute-start.21 = (f32[1,16,128]{2,1,0:T(8,128)S(1)}, f32[1,16,128]{2,1,0:T(8,128)S(1)}, u32[]{:S(2)}, u32[]{:S(2)}) collective-permute-start(f32[1,16,128]{2,1,0:T(8,128)S(1)} %get-tuple-element.667), channel_id=1, source_target_pairs={{0,16},{16,32},{32,48},{48,64},{64,80},{80,96},{96,112},{112,128},... | collective-permute-start | bytes 24584 | tf_op jit(solution)/shard_map/ppermute | solution.py:47
  121.6 8.3 %collective-permute-start.20 = (f32[1,16,128]{2,1,0:T(8,128)S(1)}, f32[1,16,128]{2,1,0:T(8,128)S(1)}, u32[]{:S(2)}, u32[]{:S(2)}) collective-permute-start(f32[1,16,128]{2,1,0:T(8,128)S(1)} %get-tuple-element.666), channel_id=1, source_target_pairs={{16,0},{32,16},{48,32},{64,48},{80,64},{96,80},{112,96},{128,112},... | collective-permute-start | bytes 24584 | tf_op jit(solution)/shard_map/ppermute | solution.py:48
  130.0 7.2 %collective-permute-start.23 = (f32[6,1,128]{2,1,0:T(1,128)S(1)}, f32[6,1,128]{2,1,0:T(1,128)S(1)}, u32[]{:S(2)}, u32[]{:S(2)}) collective-permute-start(f32[6,1,128]{2,1,0:T(1,128)S(1)} %get-tuple-element.608), channel_id=1, source_target_pairs={{0,1},{1,2},{2,3},{3,4},{4,5},{5,6},{6,7},{7,8},{8,9},{9,10},{10,1... | collective-permute-start | bytes 9224 | tf_op jit(solution)/shard_map/ppermute | solution.py:47
  131.9 6.4 %collective-permute-start.22 = (f32[6,1,128]{2,1,0:T(1,128)S(1)}, f32[6,1,128]{2,1,0:T(1,128)S(1)}, u32[]{:S(2)}, u32[]{:S(2)}) collective-permute-start(f32[6,1,128]{2,1,0:T(1,128)S(1)} %get-tuple-element.609), channel_id=1, source_target_pairs={{1,0},{2,1},{3,2},{4,3},{5,4},{6,5},{7,6},{8,7},{9,8},{10,9},{11,1... | collective-permute-start | bytes 9224 | tf_op jit(solution)/shard_map/ppermute | solution.py:48
  140.4 10.0 %collective-permute-start.25 = (f32[33,1,16,128]{3,2,1,0:T(8,128)S(1)}, f32[33,1,16,128]{3,2,1,0:T(8,128)S(1)}, u32[]{:S(2)}, u32[]{:S(2)}) collective-permute-start(f32[33,1,16,128]{3,2,1,0:T(8,128)S(1)} %get-tuple-element.557), channel_id=1, source_target_pairs={{16,0},{32,16},{48,32},{64,48},{80,64},{96,80},{112,96},{128,112},... | collective-permute-start | bytes 811016 | tf_op jit(solution)/shard_map/ppermute | solution.py:48
  146.5 11.1 %collective-permute-start.24 = (f32[33,1,16,128]{3,2,1,0:T(8,128)S(1)}, f32[33,1,16,128]{3,2,1,0:T(8,128)S(1)}, u32[]{:S(2)}, u32[]{:S(2)}) collective-permute-start(f32[33,1,16,128]{3,2,1,0:T(8,128)S(1)} %get-tuple-element.556), channel_id=1, source_target_pairs={{0,16},{16,32},{32,48},{48,64},{64,80},{80,96},{96,112},{112,128},... | collective-permute-start | bytes 811016 | tf_op jit(solution)/shard_map/ppermute | solution.py:47
  157.7 7.1 %collective-permute-start.27 = (f32[33,6,1,128]{3,2,1,0:T(1,128)S(1)}, f32[33,6,1,128]{3,2,1,0:T(1,128)S(1)}, u32[]{:S(2)}, u32[]{:S(2)}) collective-permute-start(f32[33,6,1,128]{3,2,1,0:T(1,128)S(1)} %get-tuple-element.549), channel_id=1, source_target_pairs={{1,0},{2,1},{3,2},{4,3},{5,4},{6,5},{7,6},{8,7},{9,8},{10,9},{11,1... | collective-permute-start | bytes 304136 | tf_op jit(solution)/shard_map/ppermute | solution.py:48
  162.6 7.7 %collective-permute-start.26 = (f32[33,6,1,128]{3,2,1,0:T(1,128)S(1)}, f32[33,6,1,128]{3,2,1,0:T(1,128)S(1)}, u32[]{:S(2)}, u32[]{:S(2)}) collective-permute-start(f32[33,6,1,128]{3,2,1,0:T(1,128)S(1)} %get-tuple-element.548), channel_id=1, source_target_pairs={{0,1},{1,2},{2,3},{3,4},{4,5},{5,6},{6,7},{7,8},{8,9},{9,10},{10,1... | collective-permute-start | bytes 304136 | tf_op jit(solution)/shard_map/ppermute | solution.py:47
  171.4 10.1 %collective-permute-start.29 = (f32[1,16,128]{2,1,0:T(8,128)S(1)}, f32[1,16,128]{2,1,0:T(8,128)S(1)}, u32[]{:S(2)}, u32[]{:S(2)}) collective-permute-start(f32[1,16,128]{2,1,0:T(8,128)S(1)} %get-tuple-element.657), channel_id=1, source_target_pairs={{0,16},{16,32},{32,48},{48,64},{64,80},{80,96},{96,112},{112,128},... | collective-permute-start | bytes 24584 | tf_op jit(solution)/shard_map/ppermute | solution.py:47
  173.4 8.3 %collective-permute-start.28 = (f32[1,16,128]{2,1,0:T(8,128)S(1)}, f32[1,16,128]{2,1,0:T(8,128)S(1)}, u32[]{:S(2)}, u32[]{:S(2)}) collective-permute-start(f32[1,16,128]{2,1,0:T(8,128)S(1)} %get-tuple-element.656), channel_id=1, source_target_pairs={{16,0},{32,16},{48,32},{64,48},{80,64},{96,80},{112,96},{128,112},... | collective-permute-start | bytes 24584 | tf_op jit(solution)/shard_map/ppermute | solution.py:48
  181.7 7.2 %collective-permute-start.31 = (f32[6,1,128]{2,1,0:T(1,128)S(1)}, f32[6,1,128]{2,1,0:T(1,128)S(1)}, u32[]{:S(2)}, u32[]{:S(2)}) collective-permute-start(f32[6,1,128]{2,1,0:T(1,128)S(1)} %get-tuple-element.604), channel_id=1, source_target_pairs={{0,1},{1,2},{2,3},{3,4},{4,5},{5,6},{6,7},{7,8},{8,9},{9,10},{10,1... | collective-permute-start | bytes 9224 | tf_op jit(solution)/shard_map/ppermute | solution.py:47
  183.6 6.4 %collective-permute-start.30 = (f32[6,1,128]{2,1,0:T(1,128)S(1)}, f32[6,1,128]{2,1,0:T(1,128)S(1)}, u32[]{:S(2)}, u32[]{:S(2)}) collective-permute-start(f32[6,1,128]{2,1,0:T(1,128)S(1)} %get-tuple-element.605), channel_id=1, source_target_pairs={{1,0},{2,1},{3,2},{4,3},{5,4},{6,5},{7,6},{8,7},{9,8},{10,9},{11,1... | collective-permute-start | bytes 9224 | tf_op jit(solution)/shard_map/ppermute | solution.py:48
  192.1 10.0 %collective-permute-start.33 = (f32[33,1,16,128]{3,2,1,0:T(8,128)S(1)}, f32[33,1,16,128]{3,2,1,0:T(8,128)S(1)}, u32[]{:S(2)}, u32[]{:S(2)}) collective-permute-start(f32[33,1,16,128]{3,2,1,0:T(8,128)S(1)} %get-tuple-element.555), channel_id=1, source_target_pairs={{16,0},{32,16},{48,32},{64,48},{80,64},{96,80},{112,96},{128,112},... | collective-permute-start | bytes 811016 | tf_op jit(solution)/shard_map/ppermute | solution.py:48
  198.2 11.1 %collective-permute-start.32 = (f32[33,1,16,128]{3,2,1,0:T(8,128)S(1)}, f32[33,1,16,128]{3,2,1,0:T(8,128)S(1)}, u32[]{:S(2)}, u32[]{:S(2)}) collective-permute-start(f32[33,1,16,128]{3,2,1,0:T(8,128)S(1)} %get-tuple-element.554), channel_id=1, source_target_pairs={{0,16},{16,32},{32,48},{48,64},{64,80},{80,96},{96,112},{112,128},... | collective-permute-start | bytes 811016 | tf_op jit(solution)/shard_map/ppermute | solution.py:47
  209.4 7.1 %collective-permute-start.35 = (f32[33,6,1,128]{3,2,1,0:T(1,128)S(1)}, f32[33,6,1,128]{3,2,1,0:T(1,128)S(1)}, u32[]{:S(2)}, u32[]{:S(2)}) collective-permute-start(f32[33,6,1,128]{3,2,1,0:T(1,128)S(1)} %get-tuple-element.547), channel_id=1, source_target_pairs={{1,0},{2,1},{3,2},{4,3},{5,4},{6,5},{7,6},{8,7},{9,8},{10,9},{11,1... | collective-permute-start | bytes 304136 | tf_op jit(solution)/shard_map/ppermute | solution.py:48
  214.3 7.7 %collective-permute-start.34 = (f32[33,6,1,128]{3,2,1,0:T(1,128)S(1)}, f32[33,6,1,128]{3,2,1,0:T(1,128)S(1)}, u32[]{:S(2)}, u32[]{:S(2)}) collective-permute-start(f32[33,6,1,128]{3,2,1,0:T(1,128)S(1)} %get-tuple-element.546), channel_id=1, source_target_pairs={{0,1},{1,2},{2,3},{3,4},{4,5},{5,6},{6,7},{7,8},{8,9},{9,10},{10,1... | collective-permute-start | bytes 304136 | tf_op jit(solution)/shard_map/ppermute | solution.py:47
  224.9 0.9 copy-start.2
where the time goes:
time: 227 us; the launch traced here: 226 us
  starting transfers between devices  137 us (60%)
  waiting for transfers between devices  62.6 us (28%)
  other arithmetic  12.8 us (6%)
  local copies, waits for them, and re-layouts  10.7 us (5%)
  between operations  2.38 us (1%)
    ppermute x18, starting transfers between devices, padded_2(): after = lax.ppermute(first, axis, down)  100 us
    ppermute x18, waiting for transfers between devices, padded_2(): before = lax.ppermute(last, axis, up)  49.4 us
    ppermute x18, starting transfers between devices, padded_2(): before = lax.ppermute(last, axis, up)  37 us
    ppermute x18, waiting for transfers between devices, padded_2(): after = lax.ppermute(first, axis, down)  13.1 us
    slice x132, local copies, waits for them, and re-layouts, shifted(): return jnp.roll(block, heading[2], axis=-1)  7.79 us
    unnamed x146, other arithmetic  6.92 us
  transfers between devices with their start and end apart: 36, of which 22 were waited for; matrix products, arithmetic and copies ran while one was open for 4% of the time, Pallas kernels for 0%

commit v1 on v0

v1 whole, which is shorter than its diff:
```python
import jax
import jax.numpy as jnp
from jax import lax
from jax.experimental import pallas as pl
from jax.experimental.pallas import tpu as pltpu
from jax.sharding import PartitionSpec as P

STEPS = 4
HALO = 2 * STEPS
PAD = 8

lattice_dirs = [
    (0, 0, 0),
    (1, 0, 0),
    (-1, 0, 0),
    (0, 1, 0),
    (0, -1, 0),
    (0, 0, 1),
    (0, 0, -1),
    (1, 1, 0),
    (-1, -1, 0),
    (1, -1, 0),
    (-1, 1, 0),
    (1, 0, 1),
    (-1, 0, -1),
    (1, 0, -1),
    (-1, 0, 1),
    (0, 1, 1),
    (0, -1, -1),
    (0, 1, -1),
    (0, -1, 1),
]
relax_red = 1.0
relax_blue = 0.7
tension = 0.1
segregation = 0.7
driving = 0.001
LANES = 128


def turn(value, amount):
    return pltpu.roll(value, amount % LANES, axis=1)


def gradient_of(tint, x, y):
    at = {(dx, dy): tint[x + dx, pl.ds(y + dy, 8), :] for dx in (-1, 0, 1) for dy in (-1, 0, 1)}
    along_x = {dy: at[1, dy] - at[-1, dy] for dy in (-1, 0, 1)}
    along_y = {dx: at[dx, 1] - at[dx, -1] for dx in (-1, 0, 1)}
    gx = (along_x[0] + along_x[0]) + (along_x[1] + along_x[-1]) + (turn(along_x[0], 1) + turn(along_x[0], -1))
    gy = (along_y[0] + along_y[0]) + (along_y[1] + along_y[-1]) + (turn(along_y[0], 1) + turn(along_y[0], -1))
    mixed = (at[0, 0] + at[0, 0]) + (at[1, 0] + at[-1, 0]) + (at[0, 1] + at[0, -1])
    gz = turn(mixed, -1) - turn(mixed, 1)
    twelfth = 1.0 / 12.0
    return (gx * twelfth, gy * twelfth, gz * twelfth), at[0, 0]


PAIRS = ((7, 0, 1, 1), (9, 0, 1, -1), (11, 0, 2, 1), (13, 0, 2, -1), (15, 1, 2, 1), (17, 1, 2, -1))


def collide_tile(pulled, density, flow, omega, mass, colour, gradient):
    ux, uy, uz = flow
    gx, gy, gz = gradient
    grad_sq = gx * gx + gy * gy + gz * gz
    part = tension / 36.0
    tensed = [part * g for g in gradient]
    if pulled is None:
        drift = [(3.0 / 36.0) * u for u in flow]
        curve = [(4.5 / 36.0) * u for u in flow]
        push = 3.0 * driving / 36.0
        level = 1.0 / 36.0
    else:
        level = omega * density * (1.0 / 36.0)
        triple = 3.0 * level
        drift = [triple * u for u in flow]
        curve = [1.5 * d for d in drift]
        push = (3.0 * driving / 36.0) * density
    square = [c * u + t * g for c, u, t, g in zip(curve, flow, tensed, gradient)]
    total = square[0] + square[1] + square[2]
    tense_sq = part * grad_sq
    even = level - total * (1.0 / 3.0) - (2.0 / 3.0) * tense_sq
    drift = [drift[0] + push, drift[1], drift[2]]
    twice_c = [curve[0] + curve[0], curve[1] + curve[1]]
    twice_t = [tensed[0] + tensed[0], tensed[1] + tensed[1]]
    cross = {
        (0, 1): twice_c[0] * uy + twice_t[0] * gy,
        (0, 2): twice_c[0] * uz + twice_t[0] * gz,
        (1, 2): twice_c[1] * uz + twice_t[1] * gz,
    }
    base = [even + s for s in square]
    rest = 12.0 * level - 4.0 * total + 16.0 * tense_sq
    post = [None] * 19
    keep = None if pulled is None else 1.0 - omega

    def put(member, symmetric, skew):
        if pulled is None:
            post[member] = symmetric + skew
            post[member + 1] = symmetric - skew
        else:
            post[member] = keep * pulled[member] + (symmetric + skew)
            post[member + 1] = keep * pulled[member + 1] + (symmetric - skew)

    post[0] = rest if pulled is None else keep * pulled[0] + rest
    for axis in range(3):
        put(1 + 2 * axis, base[axis] + base[axis], drift[axis] + drift[axis])
    for a, b, first, second in ((0, 1, 7, 9), (0, 2, 11, 13), (1, 2, 15, 17)):
        plane = base[a] + square[b]
        put(first, plane + cross[a, b], drift[a] + drift[b])
        put(second, plane - cross[a, b], drift[a] - drift[b])

    shrink = jnp.minimum(lax.rsqrt(grad_sq), 2.0)
    if mass is None:
        eighth = 0.125
        sway = [0.5 * u for u in flow]
    else:
        eighth = 0.125 * mass
        half = 0.5 * mass
        sway = [half * u for u in flow]
    tinted = eighth * colour
    sharpen = (0.5 * segregation) * (eighth - tinted * colour) * shrink
    fluxes = []
    for axis in range(3):
        slope = sway[axis] * colour + sharpen * gradient[axis]
        fluxes += [eighth + sway[axis], eighth - sway[axis], tinted + slope, tinted - slope]
    return post, fluxes


def kernel(par_ref, e_ref, a_ref, b_ref, s_ref, phase_ref, out_ref, vel, tint, mass, open_, star, flux):
    own_x, own_y = phase_ref.shape[0], phase_ref.shape[1]
    rows, cols = own_x + 2 * HALO, own_y + 2 * HALO
    for ref, origin, start in (
        (e_ref, 0, HALO),
        (a_ref, 0, par_ref[0]),
        (b_ref, 0, par_ref[1]),
        (s_ref, 0, par_ref[2]),
        (s_ref, own_x, par_ref[3]),
    ):
        for r in range(own_x):
            for y in range(0, cols, 8):
                colour = ref[0, origin + r, pl.ds(y, 8), :]
                tint[start + r, pl.ds(PAD + y, 8), :] = colour
                pore = jnp.where(colour != 0.0, 1.0, 0.0)
                open_[0, start + r, pl.ds(PAD + y, 8), :] = pore
                open_[1, start + r, pl.ds(PAD + y, 8), :] = turn(pore, 1)
                open_[2, start + r, pl.ds(PAD + y, 8), :] = turn(pore, -1)
                for c in range(3):
                    vel[c, start + r, pl.ds(y, 8), :] = ref[1 + c, origin + r, pl.ds(y, 8), :]

    def spread(low, high, groups, body):
        def row(x, carry):
            for y in groups:
                body(x, y)
            return carry

        lax.fori_loop(low, high, row, 0)

    def pull(ref, lead, member, x, y):
        cx, cy, cz = lattice_dirs[member]
        value = ref[lead, x - cx, pl.ds(PAD + y - cy, 8), :]
        return turn(value, cz) if cz else value

    def is_open(member, x, y):
        cx, cy, cz = lattice_dirs[member]
        return open_[cz % 3, x - cx, pl.ds(PAD + y - cy, 8), :] > 0.0

    def write(target, x, y, post, fluxes):
        for member in range(19):
            star[target, member, x, pl.ds(PAD + y, 8), :] = post[member]
        for k in range(12):
            flux[k, x, pl.ds(PAD + y, 8), :] = fluxes[k]

    def first(x, y):
        gradient, colour = gradient_of(tint, x, PAD + y)
        flow = [vel[c, x, pl.ds(y, 8), :] for c in range(3)]
        post, fluxes = collide_tile(None, None, flow, None, None, colour, gradient)
        write(0, x, y, post, fluxes)
        mass[x, pl.ds(PAD + y, 8), :] = jnp.ones_like(colour)

    groups_of = {1: range(0, cols, 8), 2: range(0, cols, 8), 3: range(4, cols - 4, 8), 4: range(4, cols - 4, 8)}
    spread(1, rows - 1, groups_of[1], first)

    def masses(x, y):
        amount = 0.25 * mass[x, pl.ds(PAD + y, 8), :]
        tinted = amount * tint[x, pl.ds(PAD + y, 8), :]
        for member in range(1, 7):
            axis, sign = divmod(member - 1, 2)
            back = 1 - sign
            free = is_open(member, x, y)
            for k in range(2):
                moved = jnp.where(
                    free,
                    pull(flux, 4 * axis + 2 * k + sign, member, x, y),
                    flux[4 * axis + 2 * k + back, x, pl.ds(PAD + y, 8), :],
                )
                if k == 0:
                    amount = amount + moved
                else:
                    tinted = tinted + moved
        pore = open_[0, x, pl.ds(PAD + y, 8), :] > 0.0
        return amount, jnp.where(pore, tinted / amount, 0.0), pore

    def pulled_of(source, x, y):
        values = [star[source, 0, x, pl.ds(PAD + y, 8), :]]
        for member in range(1, 19):
            other = member + 1 if member % 2 == 1 else member - 1
            values.append(
                jnp.where(
                    is_open(member, x, y),
                    pull(star.at[source], member, member, x, y),
                    star[source, other, x, pl.ds(PAD + y, 8), :],
                )
            )
        return values

    for step in range(2, STEPS + 1):
        source = (step - 2) % 2

        def phases(x, y):
            amount, colour, _ = masses(x, y)
            mass[x, pl.ds(PAD + y, 8), :] = amount
            tint[x, pl.ds(PAD + y, 8), :] = colour

        def later(x, y, source=source):
            pulled = pulled_of(source, x, y)
            gradient, colour = gradient_of(tint, x, PAD + y)
            summed = {m: pulled[m] + pulled[m + 1] for m in range(1, 19, 2)}
            gap = {m: pulled[m] - pulled[m + 1] for m in range(1, 19, 2)}
            density = pulled[0] + (
                ((summed[1] + summed[3]) + (summed[5] + summed[7]))
                + ((summed[9] + summed[11]) + (summed[13] + summed[15]))
                + summed[17]
            )
            jx = gap[1] + ((gap[7] + gap[9]) + (gap[11] + gap[13]))
            jy = gap[3] + ((gap[7] - gap[9]) + (gap[15] + gap[17]))
            jz = gap[5] + ((gap[11] - gap[13]) + (gap[15] - gap[17]))
            lighten = 1.0 / density
            flow = [jx * lighten, jy * lighten, jz * lighten]
            omega = 1.0 / (0.5 * (relax_red + relax_blue) + (0.5 * (relax_red - relax_blue)) * colour)
            post, fluxes = collide_tile(
                pulled, density, flow, omega, mass[x, pl.ds(PAD + y, 8), :], colour, gradient
            )
            write(1 - source, x, y, post, fluxes)

        spread(2 * step - 2, rows - 2 * step + 2, groups_of[step], phases)
        spread(2 * step - 1, rows - 2 * step + 1, groups_of[step], later)

    last = (STEPS - 1) % 2

    def final(x, y):
        _, colour, pore = masses(x, y)
        phase_ref[x - HALO, pl.ds(y - HALO, 8), :] = colour
        values = pulled_of(last, x, y)
        flow = [vel[c, x, pl.ds(y, 8), :] for c in range(3)]
        speed = flow[0] * flow[0] + flow[1] * flow[1] + flow[2] * flow[2]
        for member in range(19):
            weight = 1.0 / 3.0 if member == 0 else 1.0 / 18.0 if member < 7 else 1.0 / 36.0
            dot = sum(float(c) * u for c, u in zip(lattice_dirs[member], flow) if c != 0)
            start = weight * (1.0 + 3.0 * dot + 4.5 * dot * dot - 1.5 * speed)
            out_ref[member, x - HALO, pl.ds(y - HALO, 8), :] = jnp.where(pore, values[member], start)

    spread(HALO, HALO + own_x, range(HALO, HALO + own_y, 8), final)


def advance(places, own, inner, outer, partner):
    own_x, cols = own.shape[1], own.shape[2]
    own_y = cols - 2 * HALO
    rows = own_x + 2 * HALO
    wide = cols + 2 * PAD
    vmem = pl.BlockSpec(memory_space=pltpu.VMEM)
    return pl.pallas_call(
        kernel,
        out_shape=(
            jax.ShapeDtypeStruct((own_x, own_y, LANES), jnp.float32),
            jax.ShapeDtypeStruct((19, own_x, own_y, LANES), jnp.float32),
        ),
        in_specs=[pl.BlockSpec(memory_space=pltpu.SMEM)] + [vmem] * 4,
        out_specs=(vmem, vmem),
        scratch_shapes=[
            pltpu.VMEM((3, rows, cols, LANES), jnp.float32),
            pltpu.VMEM((rows, wide, LANES), jnp.float32),
            pltpu.VMEM((rows, wide, LANES), jnp.float32),
            pltpu.VMEM((3, rows, wide, LANES), jnp.float32),
            pltpu.VMEM((2, 19, rows, wide, LANES), jnp.float32),
            pltpu.VMEM((12, rows, wide, LANES), jnp.float32),
        ],
        compiler_params=pltpu.CompilerParams(vmem_limit_bytes=48 * 1024 * 1024),
    )(places, own, inner, outer, partner)


def exchange(array, axis, width, pairing):
    devices = lax.axis_size(axis)
    groups = devices // width
    moves = []
    for i in range(devices):
        group, place = divmod(i, width)
        step = 1 if group % 2 == pairing else -1
        moves.append((i, (group + step) % groups * width + place))
    return lax.ppermute(array, axis, moves)


def shards(pore_mask, phase_labels, velocity):
    own_x, own_y = pore_mask.shape[0], pore_mask.shape[1]
    slab, cross = lax.axis_index("slab"), lax.axis_index("cross")
    core, chip = slab % 2, slab // 2 % 2
    colour = jnp.where(pore_mask > 0, 2.0 * phase_labels.astype(jnp.float32) - 1.0, 0.0)
    block = jnp.concatenate([colour[None], velocity])
    low, high = block[:, :, :HALO], block[:, :, own_y - HALO :]
    odd = cross % 2 == 1
    near = exchange(jnp.where(odd, low, high), "cross", 1, 0)
    far = exchange(jnp.where(odd, high, low), "cross", 1, 1)
    own = jnp.concatenate([jnp.where(odd, near, far), block, jnp.where(odd, far, near)], axis=2)
    outer = exchange(own, "slab", 2, 1)
    inner = exchange(own, "slab", 2, 0)
    passed = jnp.where(core == chip, inner, outer)
    partner = exchange(jnp.concatenate([own, passed], axis=1), "slab", 1, 0)
    inner_at = jnp.where(chip == 0, HALO + 2 * own_x, 0)
    partner_at = jnp.where(core == 0, HALO + own_x, HALO - own_x)
    places = jnp.stack([inner_at, HALO + 2 * own_x - inner_at, partner_at, 2 * HALO - partner_at])
    return advance(places.astype(jnp.int32), own, inner, outer, partner)


def solution(mesh):
    in_specs = (P("slab", "cross", None), P("slab", "cross", None), P(None, "slab", "cross", None))
    out_specs = (P("slab", "cross", None), P(None, "slab", "cross", None))
    return jax.shard_map(shards, mesh=mesh, in_specs=in_specs, out_specs=out_specs, check_vma=False)
```

time: 227 us -> 58.8 us (0.26)
  the two profiles are of different devices: /device:TPU:32 before, /device:TPU:1 now
where the time goes in v1:
time: 58.8 us; the launch traced here: 58.6 us
  starting transfers between devices  28.2 us (48%)
  Pallas kernels  19.8 us (34%)
  waiting for transfers between devices  8.74 us (15%)
  other arithmetic  1.02 us (2%)
  between operations  0.78 us (1%)
    ppermute x5, starting transfers between devices, exchange(): return lax.ppermute(array, axis, moves)  28.2 us
    pallas_call x1, Pallas kernels, advance(): pl.pallas_call(kernel, out_shape=(jax.ShapeDtypeStruct((own_x, own_y, LAN...  19.8 us
    ppermute x5, waiting for transfers between devices, exchange(): return lax.ppermute(array, axis, moves)  8.74 us
  transfers between devices with their start and end apart: 5, of which 4 were waited for; matrix products, arithmetic and copies ran while one was open for 0% of the time, Pallas kernels for 0%

profile of v1, /device:TPU:1, one launch (start us, length us, event | category | flops | bytes accessed | tf_op | source)
XLA Modules:
  0.0 58.6 jit_solution(10611123717045389775)
XLA Ops:
  0.6 0.0 copy-start
  0.7 0.8 %select_bitcast_fusion = f32[1,4,16,128]{3,2,1,0:T(8,128)S(1)} fusion(s32[4,16,128]{2,1,0:T(8,128)} %param.4, s32[4,16,128]{2,1,0:T(8,128)} %param.3), kind=kLoop, calls=%fused_computation.7 | loop fusion | flops 40960 | bytes 98304 | tf_op jit(solution)/shard_map/broadcast_in_dim | solution.py:305
  1.5 0.1 copy-done
  1.5 4.4 %collective-permute-start = (f32[4,4,8,128]{3,2,1,0:T(8,128)S(1)}, f32[4,4,8,128]{3,2,1,0:T(8,128)S(1)}, u32[]{:S(2)}, u32[]{:S(2)}) collective-permute-start(f32[4,4,8,128]{3,2,1,0:T(8,128)S(1)} %get-tuple-element.4), channel_id=1, source_target_pairs={{0,1},{1,0},{2,3},{3,2},{4,5},{5,4},{6,7},{7,6},{8,9},{9,8},{10,11... | collective-permute-start | bytes 196616 | tf_op jit(solution)/shard_map/ppermute | solution.py:297
  5.9 10.2 %collective-permute-start.1 = (f32[4,4,8,128]{3,2,1,0:T(8,128)S(1)}, f32[4,4,8,128]{3,2,1,0:T(8,128)S(1)}, u32[]{:S(2)}, u32[]{:S(2)}) collective-permute-start(f32[4,4,8,128]{3,2,1,0:T(8,128)S(1)} %get-tuple-element.5), channel_id=1, source_target_pairs={{0,15},{1,2},{2,1},{3,4},{4,3},{5,6},{6,5},{7,8},{8,7},{9,10},{10,... | collective-permute-start | bytes 196616 | tf_op jit(solution)/shard_map/ppermute | solution.py:297
  16.1 0.0 collective-permute-done
  16.1 1.6 %collective-permute-done.1 = f32[4,4,8,128]{3,2,1,0:T(8,128)S(1)} collective-permute-done((f32[4,4,8,128]{3,2,1,0:T(8,128)S(1)}, f32[4,4,8,128]{3,2,1,0:T(8,128)S(1)}, u32[]{:S(2)}, u32[]{:S(2)}) %collective-permute-start.1) | collective-permute-done | bytes 65568 | tf_op jit(solution)/shard_map/ppermute | solution.py:297
  17.8 6.8 %collective-permute-start.3 = (f32[4,4,32,128]{3,2,1,0:T(8,128)S(1)}, f32[4,4,32,128]{3,2,1,0:T(8,128)S(1)}, u32[]{:S(2)}, u32[]{:S(2)}) collective-permute-start(f32[4,4,32,128]{3,2,1,0:T(8,128)S(1)} %pad_maximum_fusion.1.e_ref), channel_id=1, source_target_pairs={{0,480},{16,496},{32,64},{48,80},{64,32},{80,48},{96,128},{112,144... | collective-permute-start | bytes 786440 | tf_op jit(solution)/shard_map/ppermute | solution.py:297
  24.7 1.9 %collective-permute-start.2 = (f32[4,4,32,128]{3,2,1,0:T(8,128)S(1)}, f32[4,4,32,128]{3,2,1,0:T(8,128)S(1)}, u32[]{:S(2)}, u32[]{:S(2)}) collective-permute-start(f32[4,4,32,128]{3,2,1,0:T(8,128)S(1)} %pad_maximum_fusion.1.e_ref), channel_id=1, source_target_pairs={{0,32},{16,48},{32,0},{48,16},{64,96},{80,112},{96,64},{112,80},{1... | collective-permute-start | bytes 786440 | tf_op jit(solution)/shard_map/ppermute | solution.py:297
  26.6 2.8 %collective-permute-done.3.b_ref = f32[4,4,32,128]{3,2,1,0:T(8,128)S(1)} collective-permute-done((f32[4,4,32,128]{3,2,1,0:T(8,128)S(1)}, f32[4,4,32,128]{3,2,1,0:T(8,128)S(1)}, u32[]{:S(2)}, u32[]{:S(2)}) %collective-permute-start.3) | collective-permute-done | bytes 262176 | tf_op jit(solution)/shard_map/ppermute | solution.py:297
  29.4 2.9 %collective-permute-done.2.a_ref = f32[4,4,32,128]{3,2,1,0:T(8,128)S(1)} collective-permute-done((f32[4,4,32,128]{3,2,1,0:T(8,128)S(1)}, f32[4,4,32,128]{3,2,1,0:T(8,128)S(1)}, u32[]{:S(2)}, u32[]{:S(2)}) %collective-permute-start.2) | collective-permute-done | bytes 262176 | tf_op jit(solution)/shard_map/ppermute | solution.py:297
  32.4 4.9 %collective-permute-start.4 = (f32[4,8,32,128]{3,2,1,0:T(8,128)S(1)}, f32[4,8,32,128]{3,2,1,0:T(8,128)S(1)}, u32[]{:S(2)}, u32[]{:S(2)}) collective-permute-start(f32[4,8,32,128]{3,2,1,0:T(8,128)S(1)} %pad_maximum_fusion), channel_id=1, source_target_pairs={{0,16},{16,0},{32,48},{48,32},{64,80},{80,64},{96,112},{112,96},{1... | collective-permute-start | bytes 1572872 | tf_op jit(solution)/shard_map/ppermute | solution.py:297
  37.3 0.1 pad_add_fusion.par_ref
  37.4 1.4 %collective-permute-done.4.s_ref = f32[4,8,32,128]{3,2,1,0:T(8,128)S(1)} collective-permute-done((f32[4,8,32,128]{3,2,1,0:T(8,128)S(1)}, f32[4,8,32,128]{3,2,1,0:T(8,128)S(1)}, u32[]{:S(2)}, u32[]{:S(2)}) %collective-permute-start.4) | collective-permute-done | bytes 524320 | tf_op jit(solution)/shard_map/ppermute | solution.py:297
  38.8 19.8 %shard_map.50 = (f32[4,16,128]{2,1,0:T(8,128)}, f32[19,4,16,128]{3,2,1,0:T(8,128)}) custom-call(s32[4]{0:T(128)S(1)} %pad_add_fusion.par_ref, f32[4,4,32,128]{3,2,1,0:T(8,128)S(1)} %pad_maximum_fusion.1.e_ref, f32[4,4,32,128]{3,2,1,0:T(8,128)S(1)} %collective-permute-done.2.a_ref, f32[4,4,32,128]{3,2,1,0:T(8,128)S(1)} %collective-permute-done.3.b_ref, ...), custom_call_target="tpu_custom_call" | custom-call | tf_op jit(solution)/shard_map/pallas_call | solution.py:269
  (5 shorter events, 0.1 us)
Async XLA Ops:
  0.6 0.9 %copy-start = (f32[3,4,16,128]{3,2,1,0:T(8,128)S(1)}, f32[3,4,16,128]{3,2,1,0:T(8,128)}, u32[]{:S(2)}) copy-start(f32[3,4,16,128]{3,2,1,0:T(8,128)} %param.5) | copy-start | bytes 294916
  1.5 14.6 %collective-permute-start = (f32[4,4,8,128]{3,2,1,0:T(8,128)S(1)}, f32[4,4,8,128]{3,2,1,0:T(8,128)S(1)}, u32[]{:S(2)}, u32[]{:S(2)}) collective-permute-start(f32[4,4,8,128]{3,2,1,0:T(8,128)S(1)} %get-tuple-element.4), channel_id=1, source_target_pairs={{0,1},{1,0},{2,3},{3,2},{4,5},{5,4},{6,7},{7,6},{8,9},{9,8},{10,11... | collective-permute-start | bytes 196616 | tf_op jit(solution)/shard_map/ppermute | solution.py:297
  5.9 11.9 %collective-permute-start.1 = (f32[4,4,8,128]{3,2,1,0:T(8,128)S(1)}, f32[4,4,8,128]{3,2,1,0:T(8,128)S(1)}, u32[]{:S(2)}, u32[]{:S(2)}) collective-permute-start(f32[4,4,8,128]{3,2,1,0:T(8,128)S(1)} %get-tuple-element.5), channel_id=1, source_target_pairs={{0,15},{1,2},{2,1},{3,4},{4,3},{5,6},{6,5},{7,8},{8,7},{9,10},{10,... | collective-permute-start | bytes 196616 | tf_op jit(solution)/shard_map/ppermute | solution.py:297
  17.8 11.6 %collective-permute-start.3 = (f32[4,4,32,128]{3,2,1,0:T(8,128)S(1)}, f32[4,4,32,128]{3,2,1,0:T(8,128)S(1)}, u32[]{:S(2)}, u32[]{:S(2)}) collective-permute-start(f32[4,4,32,128]{3,2,1,0:T(8,128)S(1)} %pad_maximum_fusion.1.e_ref), channel_id=1, source_target_pairs={{0,480},{16,496},{32,64},{48,80},{64,32},{80,48},{96,128},{112,144... | collective-permute-start | bytes 786440 | tf_op jit(solution)/shard_map/ppermute | solution.py:297
  24.7 7.7 %collective-permute-start.2 = (f32[4,4,32,128]{3,2,1,0:T(8,128)S(1)}, f32[4,4,32,128]{3,2,1,0:T(8,128)S(1)}, u32[]{:S(2)}, u32[]{:S(2)}) collective-permute-start(f32[4,4,32,128]{3,2,1,0:T(8,128)S(1)} %pad_maximum_fusion.1.e_ref), channel_id=1, source_target_pairs={{0,32},{16,48},{32,0},{48,16},{64,96},{80,112},{96,64},{112,80},{1... | collective-permute-start | bytes 786440 | tf_op jit(solution)/shard_map/ppermute | solution.py:297
  32.4 6.4 %collective-permute-start.4 = (f32[4,8,32,128]{3,2,1,0:T(8,128)S(1)}, f32[4,8,32,128]{3,2,1,0:T(8,128)S(1)}, u32[]{:S(2)}, u32[]{:S(2)}) collective-permute-start(f32[4,8,32,128]{3,2,1,0:T(8,128)S(1)} %pad_maximum_fusion), channel_id=1, source_target_pairs={{0,16},{16,0},{32,48},{48,32},{64,80},{80,64},{96,112},{112,96},{1... | collective-permute-start | bytes 1572872 | tf_op jit(solution)/shard_map/ppermute | solution.py:297

commit v2 on v1

--- a/solution.py
+++ b/solution.py
@@ -4,6 +4,7 @@
 from jax.experimental import pallas as pl
 from jax.experimental.pallas import tpu as pltpu
 from jax.sharding import PartitionSpec as P
+
 
 STEPS = 4
 HALO = 2 * STEPS
@@ -54,11 +55,8 @@
     return (gx * twelfth, gy * twelfth, gz * twelfth), at[0, 0]
 
 
-PAIRS = ((7, 0, 1, 1), (9, 0, 1, -1), (11, 0, 2, 1), (13, 0, 2, -1), (15, 1, 2, 1), (17, 1, 2, -1))
-
-
 def collide_tile(pulled, density, flow, omega, mass, colour, gradient):
-    ux, uy, uz = flow
+    _, uy, uz = flow
     gx, gy, gz = gradient
     grad_sq = gx * gx + gy * gy + gz * gz
     part = tension / 36.0
@@ -124,7 +122,8 @@
     return post, fluxes
 
 
-def kernel(par_ref, e_ref, a_ref, b_ref, s_ref, phase_ref, out_ref, vel, tint, mass, open_, star, flux):
+def kernel(par_ref, e_ref, a_ref, b_ref, s_ref, phase_ref, out_ref, vel, open_, flux, *doubled):
+    tints, amounts, stars = doubled[0:2], doubled[2:4], doubled[4:6]
     own_x, own_y = phase_ref.shape[0], phase_ref.shape[1]
     rows, cols = own_x + 2 * HALO, own_y + 2 * HALO
     for ref, origin, start in (
@@ -137,7 +136,7 @@
         for r in range(own_x):
             for y in range(0, cols, 8):
                 colour = ref[0, origin + r, pl.ds(y, 8), :]
-                tint[start + r, pl.ds(PAD + y, 8), :] = colour
+                tints[0][start + r, pl.ds(PAD + y, 8), :] = colour
                 pore = jnp.where(colour != 0.0, 1.0, 0.0)
                 open_[0, start + r, pl.ds(PAD + y, 8), :] = pore
                 open_[1, start + r, pl.ds(PAD + y, 8), :] = turn(pore, 1)
@@ -145,13 +144,23 @@
                 for c in range(3):
                     vel[c, start + r, pl.ds(y, 8), :] = ref[1 + c, origin + r, pl.ds(y, 8), :]
 
-    def spread(low, high, groups, body):
-        def row(x, carry):
-            for y in groups:
-                body(x, y)
+    def spread(low, high, groups, body, tiles=None):
+        count = len(groups)
+        tiles = tiles or count
+
+        def some(i, carry):
+            if tiles >= count:
+                for x in range(tiles // count):
+                    for y in groups:
+                        body(low + i * (tiles // count) + x, y)
+            else:
+                parts = count // tiles
+                x, part = low + i // parts, i % parts
+                for k in range(tiles):
+                    body(x, groups[0] + 8 * (part * tiles + k))
             return carry
 
-        lax.fori_loop(low, high, row, 0)
+        lax.fori_loop(0, (high - low) * count // tiles, some, 0)
 
     def pull(ref, lead, member, x, y):
         cx, cy, cz = lattice_dirs[member]
@@ -164,23 +173,23 @@
 
     def write(target, x, y, post, fluxes):
         for member in range(19):
-            star[target, member, x, pl.ds(PAD + y, 8), :] = post[member]
+            stars[target][member, x, pl.ds(PAD + y, 8), :] = post[member]
         for k in range(12):
             flux[k, x, pl.ds(PAD + y, 8), :] = fluxes[k]
 
     def first(x, y):
-        gradient, colour = gradient_of(tint, x, PAD + y)
+        gradient, colour = gradient_of(tints[0], x, PAD + y)
         flow = [vel[c, x, pl.ds(y, 8), :] for c in range(3)]
         post, fluxes = collide_tile(None, None, flow, None, None, colour, gradient)
         write(0, x, y, post, fluxes)
-        mass[x, pl.ds(PAD + y, 8), :] = jnp.ones_like(colour)
+        amounts[0][x, pl.ds(PAD + y, 8), :] = jnp.ones_like(colour)
 
     groups_of = {1: range(0, cols, 8), 2: range(0, cols, 8), 3: range(4, cols - 4, 8), 4: range(4, cols - 4, 8)}
-    spread(1, rows - 1, groups_of[1], first)
-
-    def masses(x, y):
-        amount = 0.25 * mass[x, pl.ds(PAD + y, 8), :]
-        tinted = amount * tint[x, pl.ds(PAD + y, 8), :]
+    spread(1, rows - 1, groups_of[1], first, 4)
+
+    def masses(source, x, y):
+        amount = 0.25 * amounts[source][x, pl.ds(PAD + y, 8), :]
+        tinted = amount * tints[source][x, pl.ds(PAD + y, 8), :]
         for member in range(1, 7):
             axis, sign = divmod(member - 1, 2)
             back = 1 - sign
@@ -199,14 +208,14 @@
         return amount, jnp.where(pore, tinted / amount, 0.0), pore
 
     def pulled_of(source, x, y):
-        values = [star[source, 0, x, pl.ds(PAD + y, 8), :]]
+        values = [stars[source][0, x, pl.ds(PAD + y, 8), :]]
         for member in range(1, 19):
             other = member + 1 if member % 2 == 1 else member - 1
             values.append(
                 jnp.where(
                     is_open(member, x, y),
-                    pull(star.at[source], member, member, x, y),
-                    star[source, other, x, pl.ds(PAD + y, 8), :],
+                    pull(stars[source], member, member, x, y),
+                    stars[source][other, x, pl.ds(PAD + y, 8), :],
                 )
             )
         return values
@@ -214,14 +223,14 @@
     for step in range(2, STEPS + 1):
         source = (step - 2) % 2
 
-        def phases(x, y):
-            amount, colour, _ = masses(x, y)
-            mass[x, pl.ds(PAD + y, 8), :] = amount
-            tint[x, pl.ds(PAD + y, 8), :] = colour
+        def phases(x, y, source=source):
+            amount, colour, _ = masses(source, x, y)
+            amounts[1 - source][x, pl.ds(PAD + y, 8), :] = amount
+            tints[1 - source][x, pl.ds(PAD + y, 8), :] = colour
 
         def later(x, y, source=source):
             pulled = pulled_of(source, x, y)
-            gradient, colour = gradient_of(tint, x, PAD + y)
+            gradient, colour = gradient_of(tints[1 - source], x, PAD + y)
             summed = {m: pulled[m] + pulled[m + 1] for m in range(1, 19, 2)}
             gap = {m: pulled[m] - pulled[m + 1] for m in range(1, 19, 2)}
             density = pulled[0] + (
@@ -235,18 +244,17 @@
             lighten = 1.0 / density
             flow = [jx * lighten, jy * lighten, jz * lighten]
             omega = 1.0 / (0.5 * (relax_red + relax_blue) + (0.5 * (relax_red - relax_blue)) * colour)
-            post, fluxes = collide_tile(
-                pulled, density, flow, omega, mass[x, pl.ds(PAD + y, 8), :], colour, gradient
-            )
+            amount = amounts[1 - source][x, pl.ds(PAD + y, 8), :]
+            post, fluxes = collide_tile(pulled, density, flow, omega, amount, colour, gradient)
             write(1 - source, x, y, post, fluxes)
 
-        spread(2 * step - 2, rows - 2 * step + 2, groups_of[step], phases)
-        spread(2 * step - 1, rows - 2 * step + 1, groups_of[step], later)
+        spread(2 * step - 2, rows - 2 * step + 2, groups_of[step], phases, 16 if step == 2 else 12)
+        spread(2 * step - 1, rows - 2 * step + 1, groups_of[step], later, len(groups_of[step]))
 
     last = (STEPS - 1) % 2
 
     def final(x, y):
-        _, colour, pore = masses(x, y)
+        _, colour, pore = masses(last, x, y)
         phase_ref[x - HALO, pl.ds(y - HALO, 8), :] = colour
         values = pulled_of(last, x, y)
         flow = [vel[c, x, pl.ds(y, 8), :] for c in range(3)]
@@ -276,12 +284,11 @@
         out_specs=(vmem, vmem),
         scratch_shapes=[
             pltpu.VMEM((3, rows, cols, LANES), jnp.float32),
-            pltpu.VMEM((rows, wide, LANES), jnp.float32),
-            pltpu.VMEM((rows, wide, LANES), jnp.float32),
             pltpu.VMEM((3, rows, wide, LANES), jnp.float32),
-            pltpu.VMEM((2, 19, rows, wide, LANES), jnp.float32),
             pltpu.VMEM((12, rows, wide, LANES), jnp.float32),
-        ],
+        ]
+        + [pltpu.VMEM((rows, wide, LANES), jnp.float32)] * 4
+        + [pltpu.VMEM((19, rows, wide, LANES), jnp.float32)] * 2,
         compiler_params=pltpu.CompilerParams(vmem_limit_bytes=48 * 1024 * 1024),
     )(places, own, inner, outer, partner)
 
@@ -297,19 +304,22 @@
     return lax.ppermute(array, axis, moves)
 
 
+def shift(array, axis, step):
+    devices = lax.axis_size(axis)
+    return lax.ppermute(array, axis, [(i, (i + step) % devices) for i in range(devices)])
+
+
 def shards(pore_mask, phase_labels, velocity):
     own_x, own_y = pore_mask.shape[0], pore_mask.shape[1]
-    slab, cross = lax.axis_index("slab"), lax.axis_index("cross")
+    slab = lax.axis_index("slab")
     core, chip = slab % 2, slab // 2 % 2
     colour = jnp.where(pore_mask > 0, 2.0 * phase_labels.astype(jnp.float32) - 1.0, 0.0)
     block = jnp.concatenate([colour[None], velocity])
-    low, high = block[:, :, :HALO], block[:, :, own_y - HALO :]
-    odd = cross % 2 == 1
-    near = exchange(jnp.where(odd, low, high), "cross", 1, 0)
-    far = exchange(jnp.where(odd, high, low), "cross", 1, 1)
-    own = jnp.concatenate([jnp.where(odd, near, far), block, jnp.where(odd, far, near)], axis=2)
+    before = shift(block[:, :, own_y - HALO :], "cross", 1)
+    after = shift(block[:, :, :HALO], "cross", -1)
+    own = jnp.concatenate([before, block, after], axis=2)
+    inner = exchange(own, "slab", 2, 0)
     outer = exchange(own, "slab", 2, 1)
-    inner = exchange(own, "slab", 2, 0)
     passed = jnp.where(core == chip, inner, outer)
     partner = exchange(jnp.concatenate([own, passed], axis=1), "slab", 1, 0)
     inner_at = jnp.where(chip == 0, HALO + 2 * own_x, 0)

time: 58.8 us -> 50.4 us (0.86)
  Pallas kernels: 19.8 us -> 12.3 us
  starting transfers between devices: 28.2 us -> 27.2 us
    ppermute x5 -> x3, starting transfers between devices: 28.2 us -> 13.3 us  [exchange(): return lax.ppermute(array, axis, moves)]
    ppermute x0 -> x2, starting transfers between devices: none -> 13.9 us  [shift(): lax.ppermute(array, axis, [(i, (i + step) % devices) for i in range(devic...]
    pallas_call x1, Pallas kernels: 19.8 us -> 12.3 us  [advance(): pl.pallas_call(kernel, out_shape=(jax.ShapeDtypeStruct((own_x, own_y, LAN...]
    ppermute x5 -> x3, waiting for transfers between devices: 8.74 us -> 7.4 us  [exchange(): return lax.ppermute(array, axis, moves)]
    ppermute x0 -> x2, waiting for transfers between devices: none -> 1.3 us  [shift(): lax.ppermute(array, axis, [(i, (i + step) % devices) for i in range(devic...]
where the time goes in v2:
time: 50.4 us; the launch traced here: 50.1 us
  starting transfers between devices  27.2 us (54%)
  Pallas kernels  12.3 us (24%)
  waiting for transfers between devices  8.71 us (17%)
  other arithmetic  1 us (2%)
  between operations  0.76 us (2%)
    ppermute x2, starting transfers between devices, shift(): lax.ppermute(array, axis, [(i, (i + step) % devices) for i in range(devic...  13.9 us
    ppermute x3, starting transfers between devices, exchange(): return lax.ppermute(array, axis, moves)  13.3 us
    pallas_call x1, Pallas kernels, advance(): pl.pallas_call(kernel, out_shape=(jax.ShapeDtypeStruct((own_x, own_y, LAN...  12.3 us
    ppermute x3, waiting for transfers between devices, exchange(): return lax.ppermute(array, axis, moves)  7.4 us
    ppermute x2, waiting for transfers between devices, shift(): lax.ppermute(array, axis, [(i, (i + step) % devices) for i in range(devic...  1.3 us
  transfers between devices with their start and end apart: 5, of which 4 were waited for; matrix products, arithmetic and copies ran while one was open for 0% of the time, Pallas kernels for 0%

profile of v2, /device:TPU:1, one launch (start us, length us, event | category | flops | bytes accessed | tf_op | source)
XLA Modules:
  0.0 50.1 jit_solution(1648015320443600991)
XLA Ops:
  0.6 0.0 copy-start
  0.6 0.8 %select_bitcast_fusion = f32[1,4,16,128]{3,2,1,0:T(8,128)S(1)} fusion(s32[4,16,128]{2,1,0:T(8,128)} %param.4, s32[4,16,128]{2,1,0:T(8,128)} %param.3), kind=kLoop, calls=%fused_computation.7 | loop fusion | flops 40960 | bytes 98304 | tf_op jit(solution)/shard_map/broadcast_in_dim | solution.py:317
  1.5 0.1 copy-done
  1.6 4.4 %collective-permute-start = (f32[4,4,8,128]{3,2,1,0:T(8,128)S(1)}, f32[4,4,8,128]{3,2,1,0:T(8,128)S(1)}, u32[]{:S(2)}, u32[]{:S(2)}) collective-permute-start(f32[4,4,8,128]{3,2,1,0:T(8,128)S(1)} %get-tuple-element.2), channel_id=1, source_target_pairs={{0,1},{1,2},{2,3},{3,4},{4,5},{5,6},{6,7},{7,8},{8,9},{9,10},{10,1... | collective-permute-start | bytes 196616 | tf_op jit(solution)/shard_map/ppermute | solution.py:309
  5.9 9.5 %collective-permute-start.1 = (f32[4,4,8,128]{3,2,1,0:T(8,128)S(1)}, f32[4,4,8,128]{3,2,1,0:T(8,128)S(1)}, u32[]{:S(2)}, u32[]{:S(2)}) collective-permute-start(f32[4,4,8,128]{3,2,1,0:T(8,128)S(1)} %get-tuple-element.3), channel_id=1, source_target_pairs={{0,15},{1,0},{2,1},{3,2},{4,3},{5,4},{6,5},{7,6},{8,7},{9,8},{10,9... | collective-permute-start | bytes 196616 | tf_op jit(solution)/shard_map/ppermute | solution.py:309
  15.4 0.0 collective-permute-done
  15.5 1.3 %collective-permute-done.1 = f32[4,4,8,128]{3,2,1,0:T(8,128)S(1)} collective-permute-done((f32[4,4,8,128]{3,2,1,0:T(8,128)S(1)}, f32[4,4,8,128]{3,2,1,0:T(8,128)S(1)}, u32[]{:S(2)}, u32[]{:S(2)}) %collective-permute-start.1) | collective-permute-done | bytes 65568 | tf_op jit(solution)/shard_map/ppermute | solution.py:309
  16.8 6.8 %collective-permute-start.3 = (f32[4,4,32,128]{3,2,1,0:T(8,128)S(1)}, f32[4,4,32,128]{3,2,1,0:T(8,128)S(1)}, u32[]{:S(2)}, u32[]{:S(2)}) collective-permute-start(f32[4,4,32,128]{3,2,1,0:T(8,128)S(1)} %pad_maximum_fusion.1.e_ref), channel_id=1, source_target_pairs={{0,480},{16,496},{32,64},{48,80},{64,32},{80,48},{96,128},{112,144... | collective-permute-start | bytes 786440 | tf_op jit(solution)/shard_map/ppermute | solution.py:304
  23.6 1.9 %collective-permute-start.2 = (f32[4,4,32,128]{3,2,1,0:T(8,128)S(1)}, f32[4,4,32,128]{3,2,1,0:T(8,128)S(1)}, u32[]{:S(2)}, u32[]{:S(2)}) collective-permute-start(f32[4,4,32,128]{3,2,1,0:T(8,128)S(1)} %pad_maximum_fusion.1.e_ref), channel_id=1, source_target_pairs={{0,32},{16,48},{32,0},{48,16},{64,96},{80,112},{96,64},{112,80},{1... | collective-permute-start | bytes 786440 | tf_op jit(solution)/shard_map/ppermute | solution.py:304
  25.6 3.0 %collective-permute-done.3.b_ref = f32[4,4,32,128]{3,2,1,0:T(8,128)S(1)} collective-permute-done((f32[4,4,32,128]{3,2,1,0:T(8,128)S(1)}, f32[4,4,32,128]{3,2,1,0:T(8,128)S(1)}, u32[]{:S(2)}, u32[]{:S(2)}) %collective-permute-start.3) | collective-permute-done | bytes 262176 | tf_op jit(solution)/shard_map/ppermute | solution.py:304
  28.6 2.9 %collective-permute-done.2.a_ref = f32[4,4,32,128]{3,2,1,0:T(8,128)S(1)} collective-permute-done((f32[4,4,32,128]{3,2,1,0:T(8,128)S(1)}, f32[4,4,32,128]{3,2,1,0:T(8,128)S(1)}, u32[]{:S(2)}, u32[]{:S(2)}) %collective-permute-start.2) | collective-permute-done | bytes 262176 | tf_op jit(solution)/shard_map/ppermute | solution.py:304
  31.7 4.6 %collective-permute-start.4 = (f32[4,8,32,128]{3,2,1,0:T(8,128)S(1)}, f32[4,8,32,128]{3,2,1,0:T(8,128)S(1)}, u32[]{:S(2)}, u32[]{:S(2)}) collective-permute-start(f32[4,8,32,128]{3,2,1,0:T(8,128)S(1)} %pad_maximum_fusion), channel_id=1, source_target_pairs={{0,16},{16,0},{32,48},{48,32},{64,80},{80,64},{96,112},{112,96},{1... | collective-permute-start | bytes 1572872 | tf_op jit(solution)/shard_map/ppermute | solution.py:304
  36.3 0.1 pad_add_fusion.par_ref
  36.3 1.4 %collective-permute-done.4.s_ref = f32[4,8,32,128]{3,2,1,0:T(8,128)S(1)} collective-permute-done((f32[4,8,32,128]{3,2,1,0:T(8,128)S(1)}, f32[4,8,32,128]{3,2,1,0:T(8,128)S(1)}, u32[]{:S(2)}, u32[]{:S(2)}) %collective-permute-start.4) | collective-permute-done | bytes 524320 | tf_op jit(solution)/shard_map/ppermute | solution.py:304
  37.8 12.3 %shard_map.50 = (f32[4,16,128]{2,1,0:T(8,128)}, f32[19,4,16,128]{3,2,1,0:T(8,128)}) custom-call(s32[4]{0:T(128)S(1)} %pad_add_fusion.par_ref, f32[4,4,32,128]{3,2,1,0:T(8,128)S(1)} %pad_maximum_fusion.1.e_ref, f32[4,4,32,128]{3,2,1,0:T(8,128)S(1)} %collective-permute-done.2.a_ref, f32[4,4,32,128]{3,2,1,0:T(8,128)S(1)} %collective-permute-done.3.b_ref, ...), custom_call_target="tpu_custom_call" | custom-call | tf_op jit(solution)/shard_map/pallas_call | solution.py:277
  (4 shorter events, 0.1 us)
Async XLA Ops:
  0.6 0.9 %copy-start = (f32[3,4,16,128]{3,2,1,0:T(8,128)S(1)}, f32[3,4,16,128]{3,2,1,0:T(8,128)}, u32[]{:S(2)}) copy-start(f32[3,4,16,128]{3,2,1,0:T(8,128)} %param.5) | copy-start | bytes 294916
  1.6 13.9 %collective-permute-start = (f32[4,4,8,128]{3,2,1,0:T(8,128)S(1)}, f32[4,4,8,128]{3,2,1,0:T(8,128)S(1)}, u32[]{:S(2)}, u32[]{:S(2)}) collective-permute-start(f32[4,4,8,128]{3,2,1,0:T(8,128)S(1)} %get-tuple-element.2), channel_id=1, source_target_pairs={{0,1},{1,2},{2,3},{3,4},{4,5},{5,6},{6,7},{7,8},{8,9},{9,10},{10,1... | collective-permute-start | bytes 196616 | tf_op jit(solution)/shard_map/ppermute | solution.py:309
  5.9 10.8 %collective-permute-start.1 = (f32[4,4,8,128]{3,2,1,0:T(8,128)S(1)}, f32[4,4,8,128]{3,2,1,0:T(8,128)S(1)}, u32[]{:S(2)}, u32[]{:S(2)}) collective-permute-start(f32[4,4,8,128]{3,2,1,0:T(8,128)S(1)} %get-tuple-element.3), channel_id=1, source_target_pairs={{0,15},{1,0},{2,1},{3,2},{4,3},{5,4},{6,5},{7,6},{8,7},{9,8},{10,9... | collective-permute-start | bytes 196616 | tf_op jit(solution)/shard_map/ppermute | solution.py:309
  16.8 11.9 %collective-permute-start.3 = (f32[4,4,32,128]{3,2,1,0:T(8,128)S(1)}, f32[4,4,32,128]{3,2,1,0:T(8,128)S(1)}, u32[]{:S(2)}, u32[]{:S(2)}) collective-permute-start(f32[4,4,32,128]{3,2,1,0:T(8,128)S(1)} %pad_maximum_fusion.1.e_ref), channel_id=1, source_target_pairs={{0,480},{16,496},{32,64},{48,80},{64,32},{80,48},{96,128},{112,144... | collective-permute-start | bytes 786440 | tf_op jit(solution)/shard_map/ppermute | solution.py:304
  23.6 7.9 %collective-permute-start.2 = (f32[4,4,32,128]{3,2,1,0:T(8,128)S(1)}, f32[4,4,32,128]{3,2,1,0:T(8,128)S(1)}, u32[]{:S(2)}, u32[]{:S(2)}) collective-permute-start(f32[4,4,32,128]{3,2,1,0:T(8,128)S(1)} %pad_maximum_fusion.1.e_ref), channel_id=1, source_target_pairs={{0,32},{16,48},{32,0},{48,16},{64,96},{80,112},{96,64},{112,80},{1... | collective-permute-start | bytes 786440 | tf_op jit(solution)/shard_map/ppermute | solution.py:304
  31.7 6.1 %collective-permute-start.4 = (f32[4,8,32,128]{3,2,1,0:T(8,128)S(1)}, f32[4,8,32,128]{3,2,1,0:T(8,128)S(1)}, u32[]{:S(2)}, u32[]{:S(2)}) collective-permute-start(f32[4,8,32,128]{3,2,1,0:T(8,128)S(1)} %pad_maximum_fusion), channel_id=1, source_target_pairs={{0,16},{16,0},{32,48},{48,32},{64,80},{80,64},{96,112},{112,96},{1... | collective-permute-start | bytes 1572872 | tf_op jit(solution)/shard_map/ppermute | solution.py:304

commit v3 on v2

--- a/solution.py
+++ b/solution.py
@@ -37,6 +37,7 @@
 segregation = 0.7
 driving = 0.001
 LANES = 128
+SEALED = -3.0e38
 
 
 def turn(value, amount):
@@ -51,21 +52,20 @@
     gy = (along_y[0] + along_y[0]) + (along_y[1] + along_y[-1]) + (turn(along_y[0], 1) + turn(along_y[0], -1))
     mixed = (at[0, 0] + at[0, 0]) + (at[1, 0] + at[-1, 0]) + (at[0, 1] + at[0, -1])
     gz = turn(mixed, -1) - turn(mixed, 1)
-    twelfth = 1.0 / 12.0
-    return (gx * twelfth, gy * twelfth, gz * twelfth), at[0, 0]
+    return (gx, gy, gz), at[0, 0]
 
 
 def collide_tile(pulled, density, flow, omega, mass, colour, gradient):
     _, uy, uz = flow
     gx, gy, gz = gradient
     grad_sq = gx * gx + gy * gy + gz * gz
-    part = tension / 36.0
+    part = tension / 36.0 / 144.0
     tensed = [part * g for g in gradient]
     if pulled is None:
         drift = [(3.0 / 36.0) * u for u in flow]
         curve = [(4.5 / 36.0) * u for u in flow]
         push = 3.0 * driving / 36.0
-        level = 1.0 / 36.0
+        level = jnp.where(colour != 0.0, 1.0 / 36.0, jnp.nan)
     else:
         level = omega * density * (1.0 / 36.0)
         triple = 3.0 * level
@@ -74,8 +74,8 @@
         push = (3.0 * driving / 36.0) * density
     square = [c * u + t * g for c, u, t, g in zip(curve, flow, tensed, gradient)]
     total = square[0] + square[1] + square[2]
-    tense_sq = part * grad_sq
-    even = level - total * (1.0 / 3.0) - (2.0 / 3.0) * tense_sq
+    tense_sq = (2.0 * part) * grad_sq
+    even = level - (1.0 / 3.0) * (total + tense_sq)
     drift = [drift[0] + push, drift[1], drift[2]]
     twice_c = [curve[0] + curve[0], curve[1] + curve[1]]
     twice_t = [tensed[0] + tensed[0], tensed[1] + tensed[1]]
@@ -85,7 +85,7 @@
         (1, 2): twice_c[1] * uz + twice_t[1] * gz,
     }
     base = [even + s for s in square]
-    rest = 12.0 * level - 4.0 * total + 16.0 * tense_sq
+    rest = 12.0 * (even + tense_sq)
     post = [None] * 19
     keep = None if pulled is None else 1.0 - omega
 
@@ -105,9 +105,9 @@
         put(first, plane + cross[a, b], drift[a] + drift[b])
         put(second, plane - cross[a, b], drift[a] - drift[b])
 
-    shrink = jnp.minimum(lax.rsqrt(grad_sq), 2.0)
+    shrink = jnp.minimum(lax.rsqrt(grad_sq), 2.0 / 12.0)
     if mass is None:
-        eighth = 0.125
+        eighth = jnp.where(colour != 0.0, 0.125, jnp.nan)
         sway = [0.5 * u for u in flow]
     else:
         eighth = 0.125 * mass
@@ -122,8 +122,8 @@
     return post, fluxes
 
 
-def kernel(par_ref, e_ref, a_ref, b_ref, s_ref, phase_ref, out_ref, vel, open_, flux, *doubled):
-    tints, amounts, stars = doubled[0:2], doubled[2:4], doubled[4:6]
+def kernel(par_ref, e_ref, a_ref, b_ref, s_ref, phase_ref, out_ref, vel, flux, star, held, fluid, *doubled):
+    tints, amounts = doubled[0:2], doubled[2:4]
     own_x, own_y = phase_ref.shape[0], phase_ref.shape[1]
     rows, cols = own_x + 2 * HALO, own_y + 2 * HALO
     for ref, origin, start in (
@@ -135,45 +135,30 @@
     ):
         for r in range(own_x):
             for y in range(0, cols, 8):
-                colour = ref[0, origin + r, pl.ds(y, 8), :]
-                tints[0][start + r, pl.ds(PAD + y, 8), :] = colour
-                pore = jnp.where(colour != 0.0, 1.0, 0.0)
-                open_[0, start + r, pl.ds(PAD + y, 8), :] = pore
-                open_[1, start + r, pl.ds(PAD + y, 8), :] = turn(pore, 1)
-                open_[2, start + r, pl.ds(PAD + y, 8), :] = turn(pore, -1)
+                tints[0][start + r, pl.ds(PAD + y, 8), :] = ref[0, origin + r, pl.ds(y, 8), :]
                 for c in range(3):
                     vel[c, start + r, pl.ds(y, 8), :] = ref[1 + c, origin + r, pl.ds(y, 8), :]
 
     def spread(low, high, groups, body, tiles=None):
         count = len(groups)
-        tiles = tiles or count
+        height = max(1, (tiles or count) // count)
 
         def some(i, carry):
-            if tiles >= count:
-                for x in range(tiles // count):
-                    for y in groups:
-                        body(low + i * (tiles // count) + x, y)
-            else:
-                parts = count // tiles
-                x, part = low + i // parts, i % parts
-                for k in range(tiles):
-                    body(x, groups[0] + 8 * (part * tiles + k))
+            for x in range(height):
+                for y in groups:
+                    body(low + i * height + x, y)
             return carry
 
-        lax.fori_loop(0, (high - low) * count // tiles, some, 0)
+        lax.fori_loop(0, (high - low) // height, some, 0)
 
     def pull(ref, lead, member, x, y):
         cx, cy, cz = lattice_dirs[member]
         value = ref[lead, x - cx, pl.ds(PAD + y - cy, 8), :]
         return turn(value, cz) if cz else value
 
-    def is_open(member, x, y):
-        cx, cy, cz = lattice_dirs[member]
-        return open_[cz % 3, x - cx, pl.ds(PAD + y - cy, 8), :] > 0.0
-
-    def write(target, x, y, post, fluxes):
+    def write(x, y, post, fluxes):
         for member in range(19):
-            stars[target][member, x, pl.ds(PAD + y, 8), :] = post[member]
+            star[member, x, pl.ds(PAD + y, 8), :] = post[member]
         for k in range(12):
             flux[k, x, pl.ds(PAD + y, 8), :] = fluxes[k]
 
@@ -181,59 +166,45 @@
         gradient, colour = gradient_of(tints[0], x, PAD + y)
         flow = [vel[c, x, pl.ds(y, 8), :] for c in range(3)]
         post, fluxes = collide_tile(None, None, flow, None, None, colour, gradient)
-        write(0, x, y, post, fluxes)
+        write(x, y, post, fluxes)
         amounts[0][x, pl.ds(PAD + y, 8), :] = jnp.ones_like(colour)
 
-    groups_of = {1: range(0, cols, 8), 2: range(0, cols, 8), 3: range(4, cols - 4, 8), 4: range(4, cols - 4, 8)}
-    spread(1, rows - 1, groups_of[1], first, 4)
-
-    def masses(source, x, y):
+    whole, inner = range(0, cols, 8), range(4, cols - 4, 8)
+    spread(1, rows - 1, whole, first)
+
+    def streamed(source, x, y):
         amount = 0.25 * amounts[source][x, pl.ds(PAD + y, 8), :]
         tinted = amount * tints[source][x, pl.ds(PAD + y, 8), :]
-        for member in range(1, 7):
-            axis, sign = divmod(member - 1, 2)
-            back = 1 - sign
-            free = is_open(member, x, y)
-            for k in range(2):
-                moved = jnp.where(
-                    free,
-                    pull(flux, 4 * axis + 2 * k + sign, member, x, y),
-                    flux[4 * axis + 2 * k + back, x, pl.ds(PAD + y, 8), :],
-                )
-                if k == 0:
-                    amount = amount + moved
-                else:
-                    tinted = tinted + moved
-        pore = open_[0, x, pl.ds(PAD + y, 8), :] > 0.0
-        return amount, jnp.where(pore, tinted / amount, 0.0), pore
-
-    def pulled_of(source, x, y):
-        values = [stars[source][0, x, pl.ds(PAD + y, 8), :]]
+        values = [star[0, x, pl.ds(PAD + y, 8), :]]
         for member in range(1, 19):
             other = member + 1 if member % 2 == 1 else member - 1
-            values.append(
-                jnp.where(
-                    is_open(member, x, y),
-                    pull(stars[source], member, member, x, y),
-                    stars[source][other, x, pl.ds(PAD + y, 8), :],
+            moved = pull(star, member, member, x, y)
+            free = moved > SEALED
+            values.append(jnp.where(free, moved, star[other, x, pl.ds(PAD + y, 8), :]))
+            if member < 7:
+                axis, sign = divmod(member - 1, 2)
+                here, back = 4 * axis + sign, 4 * axis + 1 - sign
+                amount = amount + jnp.where(
+                    free, pull(flux, here, member, x, y), flux[back, x, pl.ds(PAD + y, 8), :]
                 )
-            )
-        return values
+                tinted = tinted + jnp.where(
+                    free, pull(flux, here + 2, member, x, y), flux[back + 2, x, pl.ds(PAD + y, 8), :]
+                )
+        pore = values[0] > SEALED
+        return amount, jnp.where(pore, tinted / amount, 0.0), pore, values
 
     for step in range(2, STEPS + 1):
-        source = (step - 2) % 2
-
-        def phases(x, y, source=source):
-            amount, colour, _ = masses(source, x, y)
+        source = step % 2
+
+        def arrive(x, y, source=source):
+            amount, colour, _, values = streamed(source, x, y)
             amounts[1 - source][x, pl.ds(PAD + y, 8), :] = amount
             tints[1 - source][x, pl.ds(PAD + y, 8), :] = colour
-
-        def later(x, y, source=source):
-            pulled = pulled_of(source, x, y)
-            gradient, colour = gradient_of(tints[1 - source], x, PAD + y)
-            summed = {m: pulled[m] + pulled[m + 1] for m in range(1, 19, 2)}
-            gap = {m: pulled[m] - pulled[m + 1] for m in range(1, 19, 2)}
-            density = pulled[0] + (
+            for member in range(19):
+                held[member, x, pl.ds(PAD + y, 8), :] = values[member]
+            summed = {m: values[m] + values[m + 1] for m in range(1, 19, 2)}
+            gap = {m: values[m] - values[m + 1] for m in range(1, 19, 2)}
+            density = values[0] + (
                 ((summed[1] + summed[3]) + (summed[5] + summed[7]))
                 + ((summed[9] + summed[11]) + (summed[13] + summed[15]))
                 + summed[17]
@@ -242,21 +213,26 @@
             jy = gap[3] + ((gap[7] - gap[9]) + (gap[15] + gap[17]))
             jz = gap[5] + ((gap[11] - gap[13]) + (gap[15] - gap[17]))
             lighten = 1.0 / density
-            flow = [jx * lighten, jy * lighten, jz * lighten]
+            for k, value in enumerate((jx * lighten, jy * lighten, jz * lighten, density)):
+                fluid[k, x, pl.ds(PAD + y, 8), :] = value
+
+        def later(x, y, source=source):
+            gradient, colour = gradient_of(tints[1 - source], x, PAD + y)
+            held_here = [held[member, x, pl.ds(PAD + y, 8), :] for member in range(19)]
+            flow = [fluid[k, x, pl.ds(PAD + y, 8), :] for k in range(3)]
+            density = fluid[3, x, pl.ds(PAD + y, 8), :]
             omega = 1.0 / (0.5 * (relax_red + relax_blue) + (0.5 * (relax_red - relax_blue)) * colour)
             amount = amounts[1 - source][x, pl.ds(PAD + y, 8), :]
-            post, fluxes = collide_tile(pulled, density, flow, omega, amount, colour, gradient)
-            write(1 - source, x, y, post, fluxes)
-
-        spread(2 * step - 2, rows - 2 * step + 2, groups_of[step], phases, 16 if step == 2 else 12)
-        spread(2 * step - 1, rows - 2 * step + 1, groups_of[step], later, len(groups_of[step]))
-
-    last = (STEPS - 1) % 2
+            post, fluxes = collide_tile(held_here, density, flow, omega, amount, colour, gradient)
+            write(x, y, post, fluxes)
+
+        groups = whole if step == 2 else inner
+        spread(2 * step - 2, rows - 2 * step + 2, groups, arrive, 4 * len(groups))
+        spread(2 * step - 1, rows - 2 * step + 1, groups, later, 2 * len(groups))
 
     def final(x, y):
-        _, colour, pore = masses(last, x, y)
+        _, colour, pore, values = streamed((STEPS + 1) % 2, x, y)
         phase_ref[x - HALO, pl.ds(y - HALO, 8), :] = colour
-        values = pulled_of(last, x, y)
         flow = [vel[c, x, pl.ds(y, 8), :] for c in range(3)]
         speed = flow[0] * flow[0] + flow[1] * flow[1] + flow[2] * flow[2]
         for member in range(19):
@@ -284,11 +260,12 @@
         out_specs=(vmem, vmem),
         scratch_shapes=[
             pltpu.VMEM((3, rows, cols, LANES), jnp.float32),
-            pltpu.VMEM((3, rows, wide, LANES), jnp.float32),
             pltpu.VMEM((12, rows, wide, LANES), jnp.float32),
+            pltpu.VMEM((19, rows, wide, LANES), jnp.float32),
+            pltpu.VMEM((19, rows, wide, LANES), jnp.float32),
+            pltpu.VMEM((4, rows, wide, LANES), jnp.float32),
         ]
-        + [pltpu.VMEM((rows, wide, LANES), jnp.float32)] * 4
-        + [pltpu.VMEM((19, rows, wide, LANES), jnp.float32)] * 2,
+        + [pltpu.VMEM((rows, wide, LANES), jnp.float32)] * 4,
         compiler_params=pltpu.CompilerParams(vmem_limit_bytes=48 * 1024 * 1024),
     )(places, own, inner, outer, partner)
 

time: 50.4 us -> 49.3 us (0.978)
  Pallas kernels: 12.3 us -> 11.3 us
    pallas_call x1, Pallas kernels: 12.3 us -> 11.3 us  [advance(): pl.pallas_call(kernel, out_shape=(jax.ShapeDtypeStruct((own_x, own_y, LAN...]
where the time goes in v3:
time: 49.3 us; the launch traced here: 49.1 us
  starting transfers between devices  27.2 us (55%)
  Pallas kernels  11.3 us (23%)
  waiting for transfers between devices  8.71 us (18%)
  other arithmetic  1 us (2%)
  between operations  0.76 us (2%)
    ppermute x2, starting transfers between devices, shift(): lax.ppermute(array, axis, [(i, (i + step) % devices) for i in range(devic...  13.9 us
    ppermute x3, starting transfers between devices, exchange(): return lax.ppermute(array, axis, moves)  13.3 us
    pallas_call x1, Pallas kernels, advance(): pl.pallas_call(kernel, out_shape=(jax.ShapeDtypeStruct((own_x, own_y, LAN...  11.3 us
    ppermute x3, waiting for transfers between devices, exchange(): return lax.ppermute(array, axis, moves)  7.4 us
    ppermute x2, waiting for transfers between devices, shift(): lax.ppermute(array, axis, [(i, (i + step) % devices) for i in range(devic...  1.3 us
  transfers between devices with their start and end apart: 5, of which 4 were waited for; matrix products, arithmetic and copies ran while one was open for 0% of the time, Pallas kernels for 0%

profile of v3, /device:TPU:1, one launch (start us, length us, event | category | flops | bytes accessed | tf_op | source)
XLA Modules:
  0.0 49.1 jit_solution(18197216982419398742)
XLA Ops:
  0.6 0.0 copy-start
  0.6 0.8 %select_bitcast_fusion = f32[1,4,16,128]{3,2,1,0:T(8,128)S(1)} fusion(s32[4,16,128]{2,1,0:T(8,128)} %param.4, s32[4,16,128]{2,1,0:T(8,128)} %param.3), kind=kLoop, calls=%fused_computation.7 | loop fusion | flops 40960 | bytes 98304 | tf_op jit(solution)/shard_map/broadcast_in_dim | solution.py:294
  1.5 0.1 copy-done
  1.6 4.4 %collective-permute-start = (f32[4,4,8,128]{3,2,1,0:T(8,128)S(1)}, f32[4,4,8,128]{3,2,1,0:T(8,128)S(1)}, u32[]{:S(2)}, u32[]{:S(2)}) collective-permute-start(f32[4,4,8,128]{3,2,1,0:T(8,128)S(1)} %get-tuple-element.2), channel_id=1, source_target_pairs={{0,1},{1,2},{2,3},{3,4},{4,5},{5,6},{6,7},{7,8},{8,9},{9,10},{10,1... | collective-permute-start | bytes 196616 | tf_op jit(solution)/shard_map/ppermute | solution.py:286
  5.9 9.5 %collective-permute-start.1 = (f32[4,4,8,128]{3,2,1,0:T(8,128)S(1)}, f32[4,4,8,128]{3,2,1,0:T(8,128)S(1)}, u32[]{:S(2)}, u32[]{:S(2)}) collective-permute-start(f32[4,4,8,128]{3,2,1,0:T(8,128)S(1)} %get-tuple-element.3), channel_id=1, source_target_pairs={{0,15},{1,0},{2,1},{3,2},{4,3},{5,4},{6,5},{7,6},{8,7},{9,8},{10,9... | collective-permute-start | bytes 196616 | tf_op jit(solution)/shard_map/ppermute | solution.py:286
  15.4 0.0 collective-permute-done
  15.5 1.3 %collective-permute-done.1 = f32[4,4,8,128]{3,2,1,0:T(8,128)S(1)} collective-permute-done((f32[4,4,8,128]{3,2,1,0:T(8,128)S(1)}, f32[4,4,8,128]{3,2,1,0:T(8,128)S(1)}, u32[]{:S(2)}, u32[]{:S(2)}) %collective-permute-start.1) | collective-permute-done | bytes 65568 | tf_op jit(solution)/shard_map/ppermute | solution.py:286
  16.8 6.8 %collective-permute-start.3 = (f32[4,4,32,128]{3,2,1,0:T(8,128)S(1)}, f32[4,4,32,128]{3,2,1,0:T(8,128)S(1)}, u32[]{:S(2)}, u32[]{:S(2)}) collective-permute-start(f32[4,4,32,128]{3,2,1,0:T(8,128)S(1)} %pad_maximum_fusion.1.e_ref), channel_id=1, source_target_pairs={{0,480},{16,496},{32,64},{48,80},{64,32},{80,48},{96,128},{112,144... | collective-permute-start | bytes 786440 | tf_op jit(solution)/shard_map/ppermute | solution.py:281
  23.6 1.9 %collective-permute-start.2 = (f32[4,4,32,128]{3,2,1,0:T(8,128)S(1)}, f32[4,4,32,128]{3,2,1,0:T(8,128)S(1)}, u32[]{:S(2)}, u32[]{:S(2)}) collective-permute-start(f32[4,4,32,128]{3,2,1,0:T(8,128)S(1)} %pad_maximum_fusion.1.e_ref), channel_id=1, source_target_pairs={{0,32},{16,48},{32,0},{48,16},{64,96},{80,112},{96,64},{112,80},{1... | collective-permute-start | bytes 786440 | tf_op jit(solution)/shard_map/ppermute | solution.py:281
  25.6 3.0 %collective-permute-done.3.b_ref = f32[4,4,32,128]{3,2,1,0:T(8,128)S(1)} collective-permute-done((f32[4,4,32,128]{3,2,1,0:T(8,128)S(1)}, f32[4,4,32,128]{3,2,1,0:T(8,128)S(1)}, u32[]{:S(2)}, u32[]{:S(2)}) %collective-permute-start.3) | collective-permute-done | bytes 262176 | tf_op jit(solution)/shard_map/ppermute | solution.py:281
  28.6 2.9 %collective-permute-done.2.a_ref = f32[4,4,32,128]{3,2,1,0:T(8,128)S(1)} collective-permute-done((f32[4,4,32,128]{3,2,1,0:T(8,128)S(1)}, f32[4,4,32,128]{3,2,1,0:T(8,128)S(1)}, u32[]{:S(2)}, u32[]{:S(2)}) %collective-permute-start.2) | collective-permute-done | bytes 262176 | tf_op jit(solution)/shard_map/ppermute | solution.py:281
  31.7 4.6 %collective-permute-start.4 = (f32[4,8,32,128]{3,2,1,0:T(8,128)S(1)}, f32[4,8,32,128]{3,2,1,0:T(8,128)S(1)}, u32[]{:S(2)}, u32[]{:S(2)}) collective-permute-start(f32[4,8,32,128]{3,2,1,0:T(8,128)S(1)} %pad_maximum_fusion), channel_id=1, source_target_pairs={{0,16},{16,0},{32,48},{48,32},{64,80},{80,64},{96,112},{112,96},{1... | collective-permute-start | bytes 1572872 | tf_op jit(solution)/shard_map/ppermute | solution.py:281
  36.3 0.1 pad_add_fusion.par_ref
  36.3 1.4 %collective-permute-done.4.s_ref = f32[4,8,32,128]{3,2,1,0:T(8,128)S(1)} collective-permute-done((f32[4,8,32,128]{3,2,1,0:T(8,128)S(1)}, f32[4,8,32,128]{3,2,1,0:T(8,128)S(1)}, u32[]{:S(2)}, u32[]{:S(2)}) %collective-permute-start.4) | collective-permute-done | bytes 524320 | tf_op jit(solution)/shard_map/ppermute | solution.py:281
  37.8 11.3 %shard_map.50 = (f32[4,16,128]{2,1,0:T(8,128)}, f32[19,4,16,128]{3,2,1,0:T(8,128)}) custom-call(s32[4]{0:T(128)S(1)} %pad_add_fusion.par_ref, f32[4,4,32,128]{3,2,1,0:T(8,128)S(1)} %pad_maximum_fusion.1.e_ref, f32[4,4,32,128]{3,2,1,0:T(8,128)S(1)} %collective-permute-done.2.a_ref, f32[4,4,32,128]{3,2,1,0:T(8,128)S(1)} %collective-permute-done.3.b_ref, ...), custom_call_target="tpu_custom_call" | custom-call | tf_op jit(solution)/shard_map/pallas_call | solution.py:253
  (4 shorter events, 0.1 us)
Async XLA Ops:
  0.6 0.9 %copy-start = (f32[3,4,16,128]{3,2,1,0:T(8,128)S(1)}, f32[3,4,16,128]{3,2,1,0:T(8,128)}, u32[]{:S(2)}) copy-start(f32[3,4,16,128]{3,2,1,0:T(8,128)} %param.5) | copy-start | bytes 294916
  1.6 13.9 %collective-permute-start = (f32[4,4,8,128]{3,2,1,0:T(8,128)S(1)}, f32[4,4,8,128]{3,2,1,0:T(8,128)S(1)}, u32[]{:S(2)}, u32[]{:S(2)}) collective-permute-start(f32[4,4,8,128]{3,2,1,0:T(8,128)S(1)} %get-tuple-element.2), channel_id=1, source_target_pairs={{0,1},{1,2},{2,3},{3,4},{4,5},{5,6},{6,7},{7,8},{8,9},{9,10},{10,1... | collective-permute-start | bytes 196616 | tf_op jit(solution)/shard_map/ppermute | solution.py:286
  5.9 10.8 %collective-permute-start.1 = (f32[4,4,8,128]{3,2,1,0:T(8,128)S(1)}, f32[4,4,8,128]{3,2,1,0:T(8,128)S(1)}, u32[]{:S(2)}, u32[]{:S(2)}) collective-permute-start(f32[4,4,8,128]{3,2,1,0:T(8,128)S(1)} %get-tuple-element.3), channel_id=1, source_target_pairs={{0,15},{1,0},{2,1},{3,2},{4,3},{5,4},{6,5},{7,6},{8,7},{9,8},{10,9... | collective-permute-start | bytes 196616 | tf_op jit(solution)/shard_map/ppermute | solution.py:286
  16.8 11.9 %collective-permute-start.3 = (f32[4,4,32,128]{3,2,1,0:T(8,128)S(1)}, f32[4,4,32,128]{3,2,1,0:T(8,128)S(1)}, u32[]{:S(2)}, u32[]{:S(2)}) collective-permute-start(f32[4,4,32,128]{3,2,1,0:T(8,128)S(1)} %pad_maximum_fusion.1.e_ref), channel_id=1, source_target_pairs={{0,480},{16,496},{32,64},{48,80},{64,32},{80,48},{96,128},{112,144... | collective-permute-start | bytes 786440 | tf_op jit(solution)/shard_map/ppermute | solution.py:281
  23.6 7.9 %collective-permute-start.2 = (f32[4,4,32,128]{3,2,1,0:T(8,128)S(1)}, f32[4,4,32,128]{3,2,1,0:T(8,128)S(1)}, u32[]{:S(2)}, u32[]{:S(2)}) collective-permute-start(f32[4,4,32,128]{3,2,1,0:T(8,128)S(1)} %pad_maximum_fusion.1.e_ref), channel_id=1, source_target_pairs={{0,32},{16,48},{32,0},{48,16},{64,96},{80,112},{96,64},{112,80},{1... | collective-permute-start | bytes 786440 | tf_op jit(solution)/shard_map/ppermute | solution.py:281
  31.7 6.1 %collective-permute-start.4 = (f32[4,8,32,128]{3,2,1,0:T(8,128)S(1)}, f32[4,8,32,128]{3,2,1,0:T(8,128)S(1)}, u32[]{:S(2)}, u32[]{:S(2)}) collective-permute-start(f32[4,8,32,128]{3,2,1,0:T(8,128)S(1)} %pad_maximum_fusion), channel_id=1, source_target_pairs={{0,16},{16,0},{32,48},{48,32},{64,80},{80,64},{96,112},{112,96},{1... | collective-permute-start | bytes 1572872 | tf_op jit(solution)/shard_map/ppermute | solution.py:281

commit v4 on v3

--- a/solution.py
+++ b/solution.py
@@ -122,22 +122,49 @@
     return post, fluxes
 
 
-def kernel(par_ref, e_ref, a_ref, b_ref, s_ref, phase_ref, out_ref, vel, flux, star, held, fluid, *doubled):
-    tints, amounts = doubled[0:2], doubled[2:4]
+def gather(ref, start, vel, tint):
+    for r in range(ref.shape[1]):
+        for y in range(0, ref.shape[2], 8):
+            tint[start + r, pl.ds(PAD + y, 8), :] = ref[0, r, pl.ds(y, 8), :]
+            for c in range(3):
+                vel[c, start + r, pl.ds(y, 8), :] = ref[1 + c, r, pl.ds(y, 8), :]
+
+
+def write(star, flux, x, y, post, fluxes):
+    for member in range(19):
+        star[member, x, pl.ds(PAD + y, 8), :] = post[member]
+    for k in range(12):
+        flux[k, x, pl.ds(PAD + y, 8), :] = fluxes[k]
+
+
+def first_row(x, vel, tint, flux, star):
+    for y in range(0, vel.shape[2], 8):
+        gradient, colour = gradient_of(tint, x, PAD + y)
+        flow = [vel[c, x, pl.ds(y, 8), :] for c in range(3)]
+        write(star, flux, x, y, *collide_tile(None, None, flow, None, None, colour, gradient))
+
+
+def early_kernel(par_ref, own_ref, inner_ref, partner_ref, vel, tint, flux, star):
+    own_x = own_ref.shape[1]
+    gather(own_ref, HALO, vel, tint)
+    gather(inner_ref, par_ref[0], vel, tint)
+    gather(partner_ref, par_ref[2], vel, tint)
+    near, side = jnp.minimum(par_ref[2], HALO) + 1, par_ref[0] + 1
+    long = 2 * own_x - 2
+
+    def row(i, carry):
+        first_row(jnp.where(i < long, near + i, side + i - long), vel, tint, flux, star)
+        return carry
+
+    lax.fori_loop(0, long + own_x - 2, row, 0)
+
+
+def kernel(par_ref, outer_ref, passed_ref, _vel, _tint, _flux, _star, phase_ref, out_ref, vel, tint, flux, star, held, fluid, *doubled):
+    tints, amounts = (tint, doubled[0]), doubled[1:3]
     own_x, own_y = phase_ref.shape[0], phase_ref.shape[1]
     rows, cols = own_x + 2 * HALO, own_y + 2 * HALO
-    for ref, origin, start in (
-        (e_ref, 0, HALO),
-        (a_ref, 0, par_ref[0]),
-        (b_ref, 0, par_ref[1]),
-        (s_ref, 0, par_ref[2]),
-        (s_ref, own_x, par_ref[3]),
-    ):
-        for r in range(own_x):
-            for y in range(0, cols, 8):
-                tints[0][start + r, pl.ds(PAD + y, 8), :] = ref[0, origin + r, pl.ds(y, 8), :]
-                for c in range(3):
-                    vel[c, start + r, pl.ds(y, 8), :] = ref[1 + c, origin + r, pl.ds(y, 8), :]
+    gather(outer_ref, par_ref[1], vel, tint)
+    gather(passed_ref, par_ref[3], vel, tint)
 
     def spread(low, high, groups, body, tiles=None):
         count = len(groups)
@@ -156,24 +183,25 @@
         value = ref[lead, x - cx, pl.ds(PAD + y - cy, 8), :]
         return turn(value, cz) if cz else value
 
-    def write(x, y, post, fluxes):
-        for member in range(19):
-            star[member, x, pl.ds(PAD + y, 8), :] = post[member]
-        for k in range(12):
-            flux[k, x, pl.ds(PAD + y, 8), :] = fluxes[k]
-
-    def first(x, y):
-        gradient, colour = gradient_of(tints[0], x, PAD + y)
-        flow = [vel[c, x, pl.ds(y, 8), :] for c in range(3)]
-        post, fluxes = collide_tile(None, None, flow, None, None, colour, gradient)
-        write(x, y, post, fluxes)
-        amounts[0][x, pl.ds(PAD + y, 8), :] = jnp.ones_like(colour)
+    near, side = jnp.minimum(par_ref[2], HALO) + 1, par_ref[0] + 1
+    long, short = 2 * own_x - 2, own_x - 2
+    low, high = jnp.minimum(near, side), jnp.maximum(near, side)
+    low_skip = jnp.where(near < side, long, short)
+
+    def row(i, carry):
+        x = 1 + i
+        x = x + jnp.where(x >= low, low_skip, 0)
+        x = x + jnp.where(x >= high, long + short - low_skip, 0)
+        first_row(x, vel, tint, flux, star)
+        return carry
+
+    lax.fori_loop(0, rows - 2 - long - short, row, 0)
 
     whole, inner = range(0, cols, 8), range(4, cols - 4, 8)
-    spread(1, rows - 1, whole, first)
 
     def streamed(source, x, y):
-        amount = 0.25 * amounts[source][x, pl.ds(PAD + y, 8), :]
+        amount = 0.25 if source is None else 0.25 * amounts[source][x, pl.ds(PAD + y, 8), :]
+        source = source or 0
         tinted = amount * tints[source][x, pl.ds(PAD + y, 8), :]
         values = [star[0, x, pl.ds(PAD + y, 8), :]]
         for member in range(1, 19):
@@ -196,8 +224,8 @@
     for step in range(2, STEPS + 1):
         source = step % 2
 
-        def arrive(x, y, source=source):
-            amount, colour, _, values = streamed(source, x, y)
+        def arrive(x, y, source=source, before=None if step == 2 else source):
+            amount, colour, _, values = streamed(before, x, y)
             amounts[1 - source][x, pl.ds(PAD + y, 8), :] = amount
             tints[1 - source][x, pl.ds(PAD + y, 8), :] = colour
             for member in range(19):
@@ -224,7 +252,7 @@
             omega = 1.0 / (0.5 * (relax_red + relax_blue) + (0.5 * (relax_red - relax_blue)) * colour)
             amount = amounts[1 - source][x, pl.ds(PAD + y, 8), :]
             post, fluxes = collide_tile(held_here, density, flow, omega, amount, colour, gradient)
-            write(x, y, post, fluxes)
+            write(star, flux, x, y, post, fluxes)
 
         groups = whole if step == 2 else inner
         spread(2 * step - 2, rows - 2 * step + 2, groups, arrive, 4 * len(groups))
@@ -244,30 +272,36 @@
     spread(HALO, HALO + own_x, range(HALO, HALO + own_y, 8), final)
 
 
-def advance(places, own, inner, outer, partner):
+def advance(places, own, inner, outer, partner, passed):
     own_x, cols = own.shape[1], own.shape[2]
     own_y = cols - 2 * HALO
-    rows = own_x + 2 * HALO
-    wide = cols + 2 * PAD
-    vmem = pl.BlockSpec(memory_space=pltpu.VMEM)
+    rows, wide = own_x + 2 * HALO, cols + 2 * PAD
+    vmem, smem = pl.BlockSpec(memory_space=pltpu.VMEM), pl.BlockSpec(memory_space=pltpu.SMEM)
+
+    def shape(*dims):
+        return jax.ShapeDtypeStruct((*dims, LANES), jnp.float32)
+
+    state_shapes = (shape(3, rows, cols), shape(rows, wide), shape(12, rows, wide), shape(19, rows, wide))
+    state = pl.pallas_call(
+        early_kernel,
+        out_shape=state_shapes,
+        in_specs=[smem] + [vmem] * 3,
+        out_specs=(vmem,) * 4,
+        compiler_params=pltpu.CompilerParams(vmem_limit_bytes=2 * 1024 * 1024),
+    )(places, own, inner, partner)
     return pl.pallas_call(
         kernel,
-        out_shape=(
-            jax.ShapeDtypeStruct((own_x, own_y, LANES), jnp.float32),
-            jax.ShapeDtypeStruct((19, own_x, own_y, LANES), jnp.float32),
-        ),
-        in_specs=[pl.BlockSpec(memory_space=pltpu.SMEM)] + [vmem] * 4,
-        out_specs=(vmem, vmem),
+        out_shape=(shape(own_x, own_y), shape(19, own_x, own_y)) + state_shapes,
+        in_specs=[smem] + [vmem] * 6,
+        out_specs=(vmem,) * 6,
         scratch_shapes=[
-            pltpu.VMEM((3, rows, cols, LANES), jnp.float32),
-            pltpu.VMEM((12, rows, wide, LANES), jnp.float32),
-            pltpu.VMEM((19, rows, wide, LANES), jnp.float32),
             pltpu.VMEM((19, rows, wide, LANES), jnp.float32),
             pltpu.VMEM((4, rows, wide, LANES), jnp.float32),
         ]
-        + [pltpu.VMEM((rows, wide, LANES), jnp.float32)] * 4,
-        compiler_params=pltpu.CompilerParams(vmem_limit_bytes=48 * 1024 * 1024),
-    )(places, own, inner, outer, partner)
+        + [pltpu.VMEM((rows, wide, LANES), jnp.float32)] * 3,
+        input_output_aliases={3: 2, 4: 3, 5: 4, 6: 5},
+        compiler_params=pltpu.CompilerParams(vmem_limit_bytes=16 * 1024 * 1024),
+    )(places, outer, passed, *state)[:2]
 
 
 def exchange(array, axis, width, pairing):
@@ -291,18 +325,18 @@
     slab = lax.axis_index("slab")
     core, chip = slab % 2, slab // 2 % 2
     colour = jnp.where(pore_mask > 0, 2.0 * phase_labels.astype(jnp.float32) - 1.0, 0.0)
-    block = jnp.concatenate([colour[None], velocity])
+    block = lax.optimization_barrier(jnp.concatenate([colour[None], velocity]))
     before = shift(block[:, :, own_y - HALO :], "cross", 1)
     after = shift(block[:, :, :HALO], "cross", -1)
     own = jnp.concatenate([before, block, after], axis=2)
     inner = exchange(own, "slab", 2, 0)
     outer = exchange(own, "slab", 2, 1)
-    passed = jnp.where(core == chip, inner, outer)
-    partner = exchange(jnp.concatenate([own, passed], axis=1), "slab", 1, 0)
+    partner = exchange(own, "slab", 1, 0)
+    passed = exchange(jnp.where(core == chip, inner, outer), "slab", 1, 0)
     inner_at = jnp.where(chip == 0, HALO + 2 * own_x, 0)
     partner_at = jnp.where(core == 0, HALO + own_x, HALO - own_x)
     places = jnp.stack([inner_at, HALO + 2 * own_x - inner_at, partner_at, 2 * HALO - partner_at])
-    return advance(places.astype(jnp.int32), own, inner, outer, partner)
+    return advance(places.astype(jnp.int32), own, inner, outer, partner, passed)
 
 
 def solution(mesh):

time: 49.3 us -> 49.1 us (level)
  waiting for transfers between devices: 8.71 us -> 2.34 us
  starting transfers between devices: 27.2 us -> 31.7 us
  other arithmetic: 1 us -> 1.82 us
  Pallas kernels: 11.3 us -> 12 us
    ppermute x3 -> x4, waiting for transfers between devices: 7.4 us -> 1.04 us  [exchange(): return lax.ppermute(array, axis, moves)]
    ppermute x3 -> x4, starting transfers between devices: 13.3 us -> 17.9 us  [exchange(): return lax.ppermute(array, axis, moves)]
    concatenate x2 -> x1, other arithmetic: 0.05 us -> 0.9 us  [shards(): block = lax.optimization_barrier(jnp.concatenate([colour[None], velocity]))]
    pallas_call x1 -> x2, Pallas kernels: 11.3 us -> 12 us  [the longest x1 10.2 us: advance(): pl.pallas_call(kernel, out_shape=(shape(own_x, own_y), shape(19, own_x, o...]
  transfers between devices with their start and end apart: 5 -> 6, of which waited for: 4 -> 2; matrix products, arithmetic and copies ran while one was open for 0% -> 0% of each run, Pallas kernels for 0% -> 4%
where the time goes in v4:
time: 49.1 us; the launch traced here: 48.7 us
  starting transfers between devices  31.7 us (65%)
  Pallas kernels  12 us (24%)
  waiting for transfers between devices  2.34 us (5%)
  other arithmetic  1.82 us (4%)
  between operations  0.79 us (2%)
    ppermute x4, starting transfers between devices, exchange(): return lax.ppermute(array, axis, moves)  17.9 us
    ppermute x2, starting transfers between devices, shift(): lax.ppermute(array, axis, [(i, (i + step) % devices) for i in range(devic...  13.9 us
    pallas_call x1, Pallas kernels, advance(): pl.pallas_call(kernel, out_shape=(shape(own_x, own_y), shape(19, own_x, o...  10.2 us
    pallas_call x1, Pallas kernels, advance(): pl.pallas_call(early_kernel, out_shape=state_shapes, in_specs=[smem] + [v...  1.83 us
    ppermute x2, waiting for transfers between devices, shift(): lax.ppermute(array, axis, [(i, (i + step) % devices) for i in range(devic...  1.3 us
    ppermute x4, waiting for transfers between devices, exchange(): return lax.ppermute(array, axis, moves)  1.04 us
  transfers between devices with their start and end apart: 6, of which 2 were waited for; matrix products, arithmetic and copies ran while one was open for 0% of the time, Pallas kernels for 4%

profile of v4, /device:TPU:1, one launch (start us, length us, event | category | flops | bytes accessed | tf_op | source)
XLA Modules:
  0.0 48.7 jit_solution(12841372835798024645)
XLA Ops:
  0.6 0.8 %select_bitcast_fusion = f32[1,4,16,128]{3,2,1,0:T(8,128)S(1)} fusion(s32[4,16,128]{2,1,0:T(8,128)} %param.4, s32[4,16,128]{2,1,0:T(8,128)} %param.3), kind=kLoop, calls=%fused_computation.3 | loop fusion | flops 40960 | bytes 98304 | tf_op jit(solution)/shard_map/broadcast_in_dim | solution.py:328
  1.4 0.9 %pad_maximum_fusion.1 = f32[4,4,16,128]{3,2,1,0:T(8,128)S(1)} fusion(f32[3,4,16,128]{3,2,1,0:T(8,128)} %param.5, f32[1,4,16,128]{3,2,1,0:T(8,128)S(1)} %select_bitcast_fusion), kind=kLoop, calls=%fused_computation.1 | loop fusion | flops 32768 | bytes 262144 | tf_op jit(solution)/shard_map/concatenate | solution.py:328
  2.3 4.4 %collective-permute-start = (f32[4,4,8,128]{3,2,1,0:T(8,128)S(1)}, f32[4,4,8,128]{3,2,1,0:T(8,128)S(1)}, u32[]{:S(2)}, u32[]{:S(2)}) collective-permute-start(f32[4,4,8,128]{3,2,1,0:T(8,128)S(1)} %get-tuple-element.14), channel_id=1, source_target_pairs={{0,1},{1,2},{2,3},{3,4},{4,5},{5,6},{6,7},{7,8},{8,9},{9,10},{10,1... | collective-permute-start | bytes 196616 | tf_op jit(solution)/shard_map/ppermute | solution.py:320
  6.7 9.5 %collective-permute-start.1 = (f32[4,4,8,128]{3,2,1,0:T(8,128)S(1)}, f32[4,4,8,128]{3,2,1,0:T(8,128)S(1)}, u32[]{:S(2)}, u32[]{:S(2)}) collective-permute-start(f32[4,4,8,128]{3,2,1,0:T(8,128)S(1)} %get-tuple-element.15), channel_id=1, source_target_pairs={{0,15},{1,0},{2,1},{3,2},{4,3},{5,4},{6,5},{7,6},{8,7},{9,8},{10,9... | collective-permute-start | bytes 196616 | tf_op jit(solution)/shard_map/ppermute | solution.py:320
  16.2 0.0 collective-permute-done
  16.2 1.3 %collective-permute-done.1 = f32[4,4,8,128]{3,2,1,0:T(8,128)S(1)} collective-permute-done((f32[4,4,8,128]{3,2,1,0:T(8,128)S(1)}, f32[4,4,8,128]{3,2,1,0:T(8,128)S(1)}, u32[]{:S(2)}, u32[]{:S(2)}) %collective-permute-start.1) | collective-permute-done | bytes 65568 | tf_op jit(solution)/shard_map/ppermute | solution.py:320
  17.6 3.1 %collective-permute-start.3 = (f32[4,4,32,128]{3,2,1,0:T(8,128)S(1)}, f32[4,4,32,128]{3,2,1,0:T(8,128)S(1)}, u32[]{:S(2)}, u32[]{:S(2)}) collective-permute-start(f32[4,4,32,128]{3,2,1,0:T(8,128)S(1)} %pad_maximum_fusion.own_ref), channel_id=1, source_target_pairs={{0,32},{16,48},{32,0},{48,16},{64,96},{80,112},{96,64},{112,80},{1... | collective-permute-start | bytes 786440 | tf_op jit(solution)/shard_map/ppermute | solution.py:315
  20.7 6.2 %collective-permute-start.2 = (f32[4,4,32,128]{3,2,1,0:T(8,128)S(1)}, f32[4,4,32,128]{3,2,1,0:T(8,128)S(1)}, u32[]{:S(2)}, u32[]{:S(2)}) collective-permute-start(f32[4,4,32,128]{3,2,1,0:T(8,128)S(1)} %pad_maximum_fusion.own_ref), channel_id=1, source_target_pairs={{0,480},{16,496},{32,64},{48,80},{64,32},{80,48},{96,128},{112,144... | collective-permute-start | bytes 786440 | tf_op jit(solution)/shard_map/ppermute | solution.py:315
  26.9 4.0 %collective-permute-start.5 = (f32[4,4,32,128]{3,2,1,0:T(8,128)S(1)}, f32[4,4,32,128]{3,2,1,0:T(8,128)S(1)}, u32[]{:S(2)}, u32[]{:S(2)}) collective-permute-start(f32[4,4,32,128]{3,2,1,0:T(8,128)S(1)} %pad_maximum_fusion.own_ref), channel_id=1, source_target_pairs={{0,16},{16,0},{32,48},{48,32},{64,80},{80,64},{96,112},{112,96},{1... | collective-permute-start | bytes 786440 | tf_op jit(solution)/shard_map/ppermute | solution.py:315
  30.9 0.0 collective-permute-done.3.inner_ref
  30.9 1.0 %collective-permute-done.2.outer_ref = f32[4,4,32,128]{3,2,1,0:T(8,128)S(1)} collective-permute-done((f32[4,4,32,128]{3,2,1,0:T(8,128)S(1)}, f32[4,4,32,128]{3,2,1,0:T(8,128)S(1)}, u32[]{:S(2)}, u32[]{:S(2)}) %collective-permute-start.2) | collective-permute-done | bytes 262176 | tf_op jit(solution)/shard_map/ppermute | solution.py:315
  32.0 4.6 %collective-permute-start.4 = (f32[4,4,32,128]{3,2,1,0:T(8,128)S(1)}, f32[4,4,32,128]{3,2,1,0:T(8,128)S(1)}, u32[]{:S(2)}, u32[]{:S(2)}) collective-permute-start(f32[4,4,32,128]{3,2,1,0:T(8,128)S(1)} %broadcast_select_fusion), channel_id=1, source_target_pairs={{0,16},{16,0},{32,48},{48,32},{64,80},{80,64},{96,112},{112,96},{1... | collective-permute-start | bytes 786440 | tf_op jit(solution)/shard_map/ppermute | solution.py:315
  36.6 0.1 pad_add_fusion.par_ref
  36.7 0.0 collective-permute-done.5.partner_ref
  36.7 1.8 %shard_map.50 = (f32[3,20,32,128]{3,2,1,0:T(8,128)S(1)}, f32[20,48,128]{2,1,0:T(8,128)S(1)}, f32[12,20,48,128]{3,2,1,0:T(8,128)S(1)}, f32[19,20,48,128]{3,2,1,0:T(8,128)S(1)}) custom-call(s32[4]{0:T(128)S(1)} %pad_add_fusion.par_ref, f32[4,4,32,128]{3,2,1,0:T(8,128)S(1)} %pad_maximum_fusion.own_ref, f32[4,4,32,128]{3,2,1,0:T(8,128)S(1)} %collective-permute-done.3.inner_ref, ...), custom_call_target="tpu_custom_call" | custom-call | tf_op jit(solution)/shard_map/pallas_call | solution.py:285
  38.5 0.0 collective-permute-done.4.passed_ref
  38.5 10.2 %shard_map.51 = (f32[4,16,128]{2,1,0:T(8,128)}, f32[19,4,16,128]{3,2,1,0:T(8,128)}, f32[3,20,32,128]{3,2,1,0:T(8,128)S(1)}, f32[20,48,128]{2,1,0:T(8,128)S(1)}, ...) custom-call(s32[4]{0:T(128)S(1)} %pad_add_fusion.par_ref, ...), custom_call_target="tpu_custom_call", output_to_operand_aliasing={{2}: (3, {}), {3}: (4, {}), {4}: (5, {}), {5}: (6, {})} | custom-call | tf_op jit(solution)/shard_map/pallas_call | solution.py:292
  (3 shorter events, 0.1 us)
Async XLA Ops:
  2.3 13.9 %collective-permute-start = (f32[4,4,8,128]{3,2,1,0:T(8,128)S(1)}, f32[4,4,8,128]{3,2,1,0:T(8,128)S(1)}, u32[]{:S(2)}, u32[]{:S(2)}) collective-permute-start(f32[4,4,8,128]{3,2,1,0:T(8,128)S(1)} %get-tuple-element.14), channel_id=1, source_target_pairs={{0,1},{1,2},{2,3},{3,4},{4,5},{5,6},{6,7},{7,8},{8,9},{9,10},{10,1... | collective-permute-start | bytes 196616 | tf_op jit(solution)/shard_map/ppermute | solution.py:320
  6.7 10.8 %collective-permute-start.1 = (f32[4,4,8,128]{3,2,1,0:T(8,128)S(1)}, f32[4,4,8,128]{3,2,1,0:T(8,128)S(1)}, u32[]{:S(2)}, u32[]{:S(2)}) collective-permute-start(f32[4,4,8,128]{3,2,1,0:T(8,128)S(1)} %get-tuple-element.15), channel_id=1, source_target_pairs={{0,15},{1,0},{2,1},{3,2},{4,3},{5,4},{6,5},{7,6},{8,7},{9,8},{10,9... | collective-permute-start | bytes 196616 | tf_op jit(solution)/shard_map/ppermute | solution.py:320
  17.6 13.4 %collective-permute-start.3 = (f32[4,4,32,128]{3,2,1,0:T(8,128)S(1)}, f32[4,4,32,128]{3,2,1,0:T(8,128)S(1)}, u32[]{:S(2)}, u32[]{:S(2)}) collective-permute-start(f32[4,4,32,128]{3,2,1,0:T(8,128)S(1)} %pad_maximum_fusion.own_ref), channel_id=1, source_target_pairs={{0,32},{16,48},{32,0},{48,16},{64,96},{80,112},{96,64},{112,80},{1... | collective-permute-start | bytes 786440 | tf_op jit(solution)/shard_map/ppermute | solution.py:315
  20.7 11.3 %collective-permute-start.2 = (f32[4,4,32,128]{3,2,1,0:T(8,128)S(1)}, f32[4,4,32,128]{3,2,1,0:T(8,128)S(1)}, u32[]{:S(2)}, u32[]{:S(2)}) collective-permute-start(f32[4,4,32,128]{3,2,1,0:T(8,128)S(1)} %pad_maximum_fusion.own_ref), channel_id=1, source_target_pairs={{0,480},{16,496},{32,64},{48,80},{64,32},{80,48},{96,128},{112,144... | collective-permute-start | bytes 786440 | tf_op jit(solution)/shard_map/ppermute | solution.py:315
  26.9 9.8 %collective-permute-start.5 = (f32[4,4,32,128]{3,2,1,0:T(8,128)S(1)}, f32[4,4,32,128]{3,2,1,0:T(8,128)S(1)}, u32[]{:S(2)}, u32[]{:S(2)}) collective-permute-start(f32[4,4,32,128]{3,2,1,0:T(8,128)S(1)} %pad_maximum_fusion.own_ref), channel_id=1, source_target_pairs={{0,16},{16,0},{32,48},{48,32},{64,80},{80,64},{96,112},{112,96},{1... | collective-permute-start | bytes 786440 | tf_op jit(solution)/shard_map/ppermute | solution.py:315
  32.0 6.5 %collective-permute-start.4 = (f32[4,4,32,128]{3,2,1,0:T(8,128)S(1)}, f32[4,4,32,128]{3,2,1,0:T(8,128)S(1)}, u32[]{:S(2)}, u32[]{:S(2)}) collective-permute-start(f32[4,4,32,128]{3,2,1,0:T(8,128)S(1)} %broadcast_select_fusion), channel_id=1, source_target_pairs={{0,16},{16,0},{32,48},{48,32},{64,80},{80,64},{96,112},{112,96},{1... | collective-permute-start | bytes 786440 | tf_op jit(solution)/shard_map/ppermute | solution.py:315

commit v5 on v4

--- a/solution.py
+++ b/solution.py
@@ -159,11 +159,23 @@
     lax.fori_loop(0, long + own_x - 2, row, 0)
 
 
-def kernel(par_ref, outer_ref, passed_ref, _vel, _tint, _flux, _star, phase_ref, out_ref, vel, tint, flux, star, held, fluid, *doubled):
+def middle_kernel(par_ref, outer_ref, _vel, _tint, _flux, _star, vel, tint, flux, star):
+    own_x = outer_ref.shape[1]
+    gather(outer_ref, par_ref[1], vel, tint)
+    joint = jnp.where(par_ref[2] > HALO, par_ref[2] + own_x, par_ref[2]) - 1
+    short = own_x - 2
+
+    def row(i, carry):
+        first_row(jnp.where(i < short, par_ref[1] + 1 + i, joint + i - short), vel, tint, flux, star)
+        return carry
+
+    lax.fori_loop(0, short + 2, row, 0)
+
+
+def kernel(par_ref, passed_ref, _vel, _tint, _flux, _star, phase_ref, out_ref, vel, tint, flux, star, held, fluid, *doubled):
     tints, amounts = (tint, doubled[0]), doubled[1:3]
     own_x, own_y = phase_ref.shape[0], phase_ref.shape[1]
     rows, cols = own_x + 2 * HALO, own_y + 2 * HALO
-    gather(outer_ref, par_ref[1], vel, tint)
     gather(passed_ref, par_ref[3], vel, tint)
 
     def spread(low, high, groups, body, tiles=None):
@@ -183,19 +195,11 @@
         value = ref[lead, x - cx, pl.ds(PAD + y - cy, 8), :]
         return turn(value, cz) if cz else value
 
-    near, side = jnp.minimum(par_ref[2], HALO) + 1, par_ref[0] + 1
-    long, short = 2 * own_x - 2, own_x - 2
-    low, high = jnp.minimum(near, side), jnp.maximum(near, side)
-    low_skip = jnp.where(near < side, long, short)
-
     def row(i, carry):
-        x = 1 + i
-        x = x + jnp.where(x >= low, low_skip, 0)
-        x = x + jnp.where(x >= high, long + short - low_skip, 0)
-        first_row(x, vel, tint, flux, star)
+        first_row(par_ref[3] - 1 + i, vel, tint, flux, star)
         return carry
 
-    lax.fori_loop(0, rows - 2 - long - short, row, 0)
+    lax.fori_loop(0, own_x + 2, row, 0)
 
     whole, inner = range(0, cols, 8), range(4, cols - 4, 8)
 
@@ -255,7 +259,7 @@
             write(star, flux, x, y, post, fluxes)
 
         groups = whole if step == 2 else inner
-        spread(2 * step - 2, rows - 2 * step + 2, groups, arrive, 4 * len(groups))
+        spread(2 * step - 2, rows - 2 * step + 2, groups, arrive, (rows - 4 * step + 4) // 2 * len(groups))
         spread(2 * step - 1, rows - 2 * step + 1, groups, later, 2 * len(groups))
 
     def final(x, y):
@@ -289,19 +293,27 @@
         out_specs=(vmem,) * 4,
         compiler_params=pltpu.CompilerParams(vmem_limit_bytes=2 * 1024 * 1024),
     )(places, own, inner, partner)
+    state = pl.pallas_call(
+        middle_kernel,
+        out_shape=state_shapes,
+        in_specs=[smem] + [vmem] * 5,
+        out_specs=(vmem,) * 4,
+        input_output_aliases={2: 0, 3: 1, 4: 2, 5: 3},
+        compiler_params=pltpu.CompilerParams(vmem_limit_bytes=2 * 1024 * 1024),
+    )(places, outer, *state)
     return pl.pallas_call(
         kernel,
         out_shape=(shape(own_x, own_y), shape(19, own_x, own_y)) + state_shapes,
-        in_specs=[smem] + [vmem] * 6,
+        in_specs=[smem] + [vmem] * 5,
         out_specs=(vmem,) * 6,
         scratch_shapes=[
             pltpu.VMEM((19, rows, wide, LANES), jnp.float32),
             pltpu.VMEM((4, rows, wide, LANES), jnp.float32),
         ]
         + [pltpu.VMEM((rows, wide, LANES), jnp.float32)] * 3,
-        input_output_aliases={3: 2, 4: 3, 5: 4, 6: 5},
+        input_output_aliases={2: 2, 3: 3, 4: 4, 5: 5},
         compiler_params=pltpu.CompilerParams(vmem_limit_bytes=16 * 1024 * 1024),
-    )(places, outer, passed, *state)[:2]
+    )(places, passed, *state)[:2]
 
 
 def exchange(array, axis, width, pairing):

time: 49.1 us -> 49.9 us (1.016)
  waiting for transfers between devices: 2.34 us -> 3.56 us
  starting transfers between devices: 31.7 us -> 30.9 us
  Pallas kernels: 12 us -> 12.5 us
    ppermute x4, waiting for transfers between devices: 1.04 us -> 2.26 us  [exchange(): return lax.ppermute(array, axis, moves)]
    pallas_call x0 -> x1, Pallas kernels: none -> 1.18 us  [advance(): pl.pallas_call(middle_kernel, out_shape=state_shapes, in_specs=[smem] + [...]
    ppermute x4, starting transfers between devices: 17.9 us -> 17 us  [exchange(): return lax.ppermute(array, axis, moves)]
    pallas_call x1, Pallas kernels: 10.2 us -> 9.46 us  [advance(): pl.pallas_call(kernel, out_shape=(shape(own_x, own_y), shape(19, own_x, o...]
  transfers between devices with their start and end apart: 6 -> 6, of which waited for: 2 -> 2; matrix products, arithmetic and copies ran while one was open for 0% -> 0% of each run, Pallas kernels for 4% -> 6%
where the time goes in v5:
time: 49.9 us; the launch traced here: 49.6 us
  starting transfers between devices  30.9 us (62%)
  Pallas kernels  12.5 us (25%)
  waiting for transfers between devices  3.56 us (7%)
  other arithmetic  1.82 us (4%)
  between operations  0.79 us (2%)
    ppermute x4, starting transfers between devices, exchange(): return lax.ppermute(array, axis, moves)  17 us
    ppermute x2, starting transfers between devices, shift(): lax.ppermute(array, axis, [(i, (i + step) % devices) for i in range(devic...  13.9 us
    pallas_call x1, Pallas kernels, advance(): pl.pallas_call(kernel, out_shape=(shape(own_x, own_y), shape(19, own_x, o...  9.46 us
    ppermute x4, waiting for transfers between devices, exchange(): return lax.ppermute(array, axis, moves)  2.26 us
    pallas_call x1, Pallas kernels, advance(): pl.pallas_call(early_kernel, out_shape=state_shapes, in_specs=[smem] + [v...  1.83 us
    ppermute x2, waiting for transfers between devices, shift(): lax.ppermute(array, axis, [(i, (i + step) % devices) for i in range(devic...  1.3 us
    pallas_call x1, Pallas kernels, advance(): pl.pallas_call(middle_kernel, out_shape=state_shapes, in_specs=[smem] + [...  1.18 us
  transfers between devices with their start and end apart: 6, of which 2 were waited for; matrix products, arithmetic and copies ran while one was open for 0% of the time, Pallas kernels for 6%

profile of v5, /device:TPU:1, one launch (start us, length us, event | category | flops | bytes accessed | tf_op | source)
XLA Modules:
  0.0 49.6 jit_solution(4191776999995805621)
XLA Ops:
  0.6 0.8 %select_bitcast_fusion = f32[1,4,16,128]{3,2,1,0:T(8,128)S(1)} fusion(s32[4,16,128]{2,1,0:T(8,128)} %param.4, s32[4,16,128]{2,1,0:T(8,128)} %param.3), kind=kLoop, calls=%fused_computation.3 | loop fusion | flops 40960 | bytes 98304 | tf_op jit(solution)/shard_map/broadcast_in_dim | solution.py:340
  1.4 0.9 %pad_maximum_fusion.1 = f32[4,4,16,128]{3,2,1,0:T(8,128)S(1)} fusion(f32[3,4,16,128]{3,2,1,0:T(8,128)} %param.5, f32[1,4,16,128]{3,2,1,0:T(8,128)S(1)} %select_bitcast_fusion), kind=kLoop, calls=%fused_computation.1 | loop fusion | flops 32768 | bytes 262144 | tf_op jit(solution)/shard_map/concatenate | solution.py:340
  2.3 4.4 %collective-permute-start = (f32[4,4,8,128]{3,2,1,0:T(8,128)S(1)}, f32[4,4,8,128]{3,2,1,0:T(8,128)S(1)}, u32[]{:S(2)}, u32[]{:S(2)}) collective-permute-start(f32[4,4,8,128]{3,2,1,0:T(8,128)S(1)} %get-tuple-element.22), channel_id=1, source_target_pairs={{0,1},{1,2},{2,3},{3,4},{4,5},{5,6},{6,7},{7,8},{8,9},{9,10},{10,1... | collective-permute-start | bytes 196616 | tf_op jit(solution)/shard_map/ppermute | solution.py:332
  6.7 9.5 %collective-permute-start.1 = (f32[4,4,8,128]{3,2,1,0:T(8,128)S(1)}, f32[4,4,8,128]{3,2,1,0:T(8,128)S(1)}, u32[]{:S(2)}, u32[]{:S(2)}) collective-permute-start(f32[4,4,8,128]{3,2,1,0:T(8,128)S(1)} %get-tuple-element.23), channel_id=1, source_target_pairs={{0,15},{1,0},{2,1},{3,2},{4,3},{5,4},{6,5},{7,6},{8,7},{9,8},{10,9... | collective-permute-start | bytes 196616 | tf_op jit(solution)/shard_map/ppermute | solution.py:332
  16.2 0.0 collective-permute-done
  16.2 1.3 %collective-permute-done.1 = f32[4,4,8,128]{3,2,1,0:T(8,128)S(1)} collective-permute-done((f32[4,4,8,128]{3,2,1,0:T(8,128)S(1)}, f32[4,4,8,128]{3,2,1,0:T(8,128)S(1)}, u32[]{:S(2)}, u32[]{:S(2)}) %collective-permute-start.1) | collective-permute-done | bytes 65568 | tf_op jit(solution)/shard_map/ppermute | solution.py:332
  17.6 6.8 %collective-permute-start.3 = (f32[4,4,32,128]{3,2,1,0:T(8,128)S(1)}, f32[4,4,32,128]{3,2,1,0:T(8,128)S(1)}, u32[]{:S(2)}, u32[]{:S(2)}) collective-permute-start(f32[4,4,32,128]{3,2,1,0:T(8,128)S(1)} %pad_maximum_fusion.own_ref), channel_id=1, source_target_pairs={{0,480},{16,496},{32,64},{48,80},{64,32},{80,48},{96,128},{112,144... | collective-permute-start | bytes 786440 | tf_op jit(solution)/shard_map/ppermute | solution.py:327
  24.4 1.9 %collective-permute-start.2 = (f32[4,4,32,128]{3,2,1,0:T(8,128)S(1)}, f32[4,4,32,128]{3,2,1,0:T(8,128)S(1)}, u32[]{:S(2)}, u32[]{:S(2)}) collective-permute-start(f32[4,4,32,128]{3,2,1,0:T(8,128)S(1)} %pad_maximum_fusion.own_ref), channel_id=1, source_target_pairs={{0,32},{16,48},{32,0},{48,16},{64,96},{80,112},{96,64},{112,80},{1... | collective-permute-start | bytes 786440 | tf_op jit(solution)/shard_map/ppermute | solution.py:327
  26.4 3.7 %collective-permute-start.5 = (f32[4,4,32,128]{3,2,1,0:T(8,128)S(1)}, f32[4,4,32,128]{3,2,1,0:T(8,128)S(1)}, u32[]{:S(2)}, u32[]{:S(2)}) collective-permute-start(f32[4,4,32,128]{3,2,1,0:T(8,128)S(1)} %pad_maximum_fusion.own_ref), channel_id=1, source_target_pairs={{0,16},{16,0},{32,48},{48,32},{64,80},{80,64},{96,112},{112,96},{1... | collective-permute-start | bytes 786440 | tf_op jit(solution)/shard_map/ppermute | solution.py:327
  30.1 0.0 collective-permute-done.3.outer_ref
  30.1 2.2 %collective-permute-done.2.inner_ref = f32[4,4,32,128]{3,2,1,0:T(8,128)S(1)} collective-permute-done((f32[4,4,32,128]{3,2,1,0:T(8,128)S(1)}, f32[4,4,32,128]{3,2,1,0:T(8,128)S(1)}, u32[]{:S(2)}, u32[]{:S(2)}) %collective-permute-start.2) | collective-permute-done | bytes 262176 | tf_op jit(solution)/shard_map/ppermute | solution.py:327
  32.4 4.6 %collective-permute-start.4 = (f32[4,4,32,128]{3,2,1,0:T(8,128)S(1)}, f32[4,4,32,128]{3,2,1,0:T(8,128)S(1)}, u32[]{:S(2)}, u32[]{:S(2)}) collective-permute-start(f32[4,4,32,128]{3,2,1,0:T(8,128)S(1)} %broadcast_select_fusion), channel_id=1, source_target_pairs={{0,16},{16,0},{32,48},{48,32},{64,80},{80,64},{96,112},{112,96},{1... | collective-permute-start | bytes 786440 | tf_op jit(solution)/shard_map/ppermute | solution.py:327
  37.0 0.1 pad_add_fusion.par_ref
  37.1 0.0 collective-permute-done.5.partner_ref
  37.1 1.8 %shard_map.50 = (f32[3,20,32,128]{3,2,1,0:T(8,128)S(1)}, f32[20,48,128]{2,1,0:T(8,128)S(1)}, f32[12,20,48,128]{3,2,1,0:T(8,128)S(1)}, f32[19,20,48,128]{3,2,1,0:T(8,128)S(1)}) custom-call(s32[4]{0:T(128)S(1)} %pad_add_fusion.par_ref, f32[4,4,32,128]{3,2,1,0:T(8,128)S(1)} %pad_maximum_fusion.own_ref, f32[4,4,32,128]{3,2,1,0:T(8,128)S(1)} %collective-permute-done.2.inner_ref, ...), custom_call_target="tpu_custom_call" | custom-call | tf_op jit(solution)/shard_map/pallas_call | solution.py:289
  38.9 1.2 %shard_map.51 = (f32[3,20,32,128]{3,2,1,0:T(8,128)S(1)}, f32[20,48,128]{2,1,0:T(8,128)S(1)}, f32[12,20,48,128]{3,2,1,0:T(8,128)S(1)}, f32[19,20,48,128]{3,2,1,0:T(8,128)S(1)}) custom-call(s32[4]{0:T(128)S(1)} %pad_add_fusion.par_ref, ...), custom_call_target="tpu_custom_call", output_to_operand_aliasing={{0}: (2, {}), {1}: (3, {}), {2}: (4, {}), {3}: (5, {})} | custom-call | tf_op jit(solution)/shard_map/pallas_call | solution.py:296
  40.1 0.0 collective-permute-done.4.passed_ref
  40.1 9.5 %shard_map.52 = (f32[4,16,128]{2,1,0:T(8,128)}, f32[19,4,16,128]{3,2,1,0:T(8,128)}, f32[3,20,32,128]{3,2,1,0:T(8,128)S(1)}, f32[20,48,128]{2,1,0:T(8,128)S(1)}, ...) custom-call(s32[4]{0:T(128)S(1)} %pad_add_fusion.par_ref, ...), custom_call_target="tpu_custom_call", output_to_operand_aliasing={{2}: (2, {}), {3}: (3, {}), {4}: (4, {}), {5}: (5, {})} | custom-call | tf_op jit(solution)/shard_map/pallas_call | solution.py:304
  (3 shorter events, 0.1 us)
Async XLA Ops:
  2.3 13.9 %collective-permute-start = (f32[4,4,8,128]{3,2,1,0:T(8,128)S(1)}, f32[4,4,8,128]{3,2,1,0:T(8,128)S(1)}, u32[]{:S(2)}, u32[]{:S(2)}) collective-permute-start(f32[4,4,8,128]{3,2,1,0:T(8,128)S(1)} %get-tuple-element.22), channel_id=1, source_target_pairs={{0,1},{1,2},{2,3},{3,4},{4,5},{5,6},{6,7},{7,8},{8,9},{9,10},{10,1... | collective-permute-start | bytes 196616 | tf_op jit(solution)/shard_map/ppermute | solution.py:332
  6.7 10.8 %collective-permute-start.1 = (f32[4,4,8,128]{3,2,1,0:T(8,128)S(1)}, f32[4,4,8,128]{3,2,1,0:T(8,128)S(1)}, u32[]{:S(2)}, u32[]{:S(2)}) collective-permute-start(f32[4,4,8,128]{3,2,1,0:T(8,128)S(1)} %get-tuple-element.23), channel_id=1, source_target_pairs={{0,15},{1,0},{2,1},{3,2},{4,3},{5,4},{6,5},{7,6},{8,7},{9,8},{10,9... | collective-permute-start | bytes 196616 | tf_op jit(solution)/shard_map/ppermute | solution.py:332
  17.6 12.5 %collective-permute-start.3 = (f32[4,4,32,128]{3,2,1,0:T(8,128)S(1)}, f32[4,4,32,128]{3,2,1,0:T(8,128)S(1)}, u32[]{:S(2)}, u32[]{:S(2)}) collective-permute-start(f32[4,4,32,128]{3,2,1,0:T(8,128)S(1)} %pad_maximum_fusion.own_ref), channel_id=1, source_target_pairs={{0,480},{16,496},{32,64},{48,80},{64,32},{80,48},{96,128},{112,144... | collective-permute-start | bytes 786440 | tf_op jit(solution)/shard_map/ppermute | solution.py:327
  24.4 7.9 %collective-permute-start.2 = (f32[4,4,32,128]{3,2,1,0:T(8,128)S(1)}, f32[4,4,32,128]{3,2,1,0:T(8,128)S(1)}, u32[]{:S(2)}, u32[]{:S(2)}) collective-permute-start(f32[4,4,32,128]{3,2,1,0:T(8,128)S(1)} %pad_maximum_fusion.own_ref), channel_id=1, source_target_pairs={{0,32},{16,48},{32,0},{48,16},{64,96},{80,112},{96,64},{112,80},{1... | collective-permute-start | bytes 786440 | tf_op jit(solution)/shard_map/ppermute | solution.py:327
  26.4 10.7 %collective-permute-start.5 = (f32[4,4,32,128]{3,2,1,0:T(8,128)S(1)}, f32[4,4,32,128]{3,2,1,0:T(8,128)S(1)}, u32[]{:S(2)}, u32[]{:S(2)}) collective-permute-start(f32[4,4,32,128]{3,2,1,0:T(8,128)S(1)} %pad_maximum_fusion.own_ref), channel_id=1, source_target_pairs={{0,16},{16,0},{32,48},{48,32},{64,80},{80,64},{96,112},{112,96},{1... | collective-permute-start | bytes 786440 | tf_op jit(solution)/shard_map/ppermute | solution.py:327
  32.4 7.7 %collective-permute-start.4 = (f32[4,4,32,128]{3,2,1,0:T(8,128)S(1)}, f32[4,4,32,128]{3,2,1,0:T(8,128)S(1)}, u32[]{:S(2)}, u32[]{:S(2)}) collective-permute-start(f32[4,4,32,128]{3,2,1,0:T(8,128)S(1)} %broadcast_select_fusion), channel_id=1, source_target_pairs={{0,16},{16,0},{32,48},{48,32},{64,80},{80,64},{96,112},{112,96},{1... | collective-permute-start | bytes 786440 | tf_op jit(solution)/shard_map/ppermute | solution.py:327
